TPU v7x, 512 devices: a whole 4x8x8 slice. The times are simulated.
512 devices in a mesh: span: 16 (over z, core), grp: 32 (over y, x).
Axes of the slice: x: 4, y: 8, z: 8, core: 2. Of those that a mesh axis runs over, the one named last changes fastest.
Arguments:
- displacement: float32 [16, 5, 32768], P('span', None, 'grp'), may hold values from -3 to 3
- velocity: float32 [16, 5, 32768], P('span', None, 'grp'), may hold values from -3 to 3
- nodal_load: float32 [16, 5, 32768], P('span', None, 'grp'), may hold values from -6 to 6
- nodal_mass: float32 [16, 32768], P('span', 'grp'), may hold values from 1 to 4
- plastic_strain: float32 [16, 512, 3, 5, 128], P('span', 'grp'), may hold values from -0.3 to 0.3
- hardening: float32 [16, 512, 5, 128], P('span', 'grp'), may hold values from 0 to 0.2
- ply_modulus: float32 [16, 512, 5, 128], P('span', 'grp'), may hold values from 0.5 to 2
- inverse_size: float32 [16, 512, 128], P('span', 'grp'), may hold values from 0.5 to 2
- cost_map: int32 [16, 512], P('span'), may hold values from 1 to 4
- migration_plan: int32 [16, 512, 1], P('span'), may hold values from 0 to 31; in each aligned block of 16 rows (0 to 15, 16 to 31, ..., all dimensions but the last counted through in order) no two rows name the same one
- block_nodes: int32 [16, 512, 256], P('span'), may hold values from 0 to 32959, as said below
- corner_slot: int32 [16, 512, 4, 128], P('span'), may hold values from 0 to 255
Outputs:
- displacement_out: float32 [16, 5, 32768], P('span', None, 'grp')
- velocity_out: float32 [16, 5, 32768], P('span', None, 'grp')
- resident_plastic: float32 [16, 1024, 3, 5, 128], P('span', 'grp')
- resident_hardening: float32 [16, 1024, 5, 128], P('span', 'grp')
Inputs may be any that keep to these rules, and one draw needn't show every extreme that they name: `migration_plan`: of the 16 blocks that start on one device (aligned blocks of 16 entries), no more than 1 name the same device. `cost_map`: newton turns of a block. `block_nodes`: block b of a span group (0 to 511) lists 256 distinct nodes from b * (64) on.
All inputs are finite; a program needn't handle non-finite values.
Results may differ from a plain program's by a relative error of at most 0.0003.
Values sent between devices are 32-bit elements; how exact they have to be, the bound alone decides.
No kernel may reach another device: no remote copies, remote signals or barrier semaphores. Data moves between devices by JAX's collectives and lax.ppermute only.
A program may use at most 64 MiB of HBM per device.

v0:
```python
import jax
import jax.numpy as jnp
from jax import lax
from jax.sharding import PartitionSpec as P

NEWTON = 4
STEPS = 4


POISSON = 0.3
YIELD = 0.1
SATURATE = 0.1
RATE = 20.0
STEP_TIME = 0.25
HIGHEST = lax.Precision.HIGHEST


def from_behind(shard, axis, by):
    size = lax.axis_size(axis)
    pairs = [(i, i + by) for i in range(size) if 0 <= i + by < size]
    return lax.ppermute(shard, axis, pairs)


def element_update(corner_disp, inverse_size, modulus, plastic, harden, costs):
    corner_a = corner_disp[:, :, 0]
    corner_b = corner_disp[:, :, 1]
    corner_c = corner_disp[:, :, 2]
    corner_d = corner_disp[:, :, 3]
    inverse = inverse_size[:, None, :]
    deriv_x = 0.5 * inverse * (corner_b + corner_c - corner_a - corner_d)
    deriv_y = 0.5 * inverse * (corner_c + corner_d - corner_a - corner_b)
    centre = 0.25 * (corner_a + corner_b + corner_c + corner_d)
    membrane = jnp.stack([deriv_x[:, 0], deriv_y[:, 1], deriv_y[:, 0] + deriv_x[:, 1]], 1)
    bending = jnp.stack([deriv_x[:, 3], deriv_y[:, 4], deriv_y[:, 3] + deriv_x[:, 4]], 1)
    transverse = jnp.stack([deriv_x[:, 2] + centre[:, 3], deriv_y[:, 2] + centre[:, 4]], 1)
    heights = jnp.array([-0.5, -0.25, 0.0, 0.25, 0.5], jnp.float32)
    through = jnp.array([1.0, 4.0, 2.0, 4.0, 1.0], jnp.float32) / 12.0
    strains = membrane[:, :, None, :] + heights[None, None, :, None] * bending[:, :, None, :]
    elastic = strains - plastic
    stiffness = modulus / (1.0 - POISSON * POISSON)
    trial_stress = jnp.stack(
        [
            stiffness * (elastic[:, 0] + POISSON * elastic[:, 1]),
            stiffness * (POISSON * elastic[:, 0] + elastic[:, 1]),
            stiffness * 0.5 * (1.0 - POISSON) * elastic[:, 2],
        ],
        1,
    )
    equivalent = jnp.sqrt(
        (trial_stress[:, 0] - 0.5 * trial_stress[:, 1]) ** 2
        + 0.75 * trial_stress[:, 1] ** 2
        + 3.0 * trial_stress[:, 2] ** 2
    )
    shear_three = 1.5 * modulus / (1.0 + POISSON)
    initial_yield = YIELD + SATURATE * (1.0 - jnp.exp(-RATE * harden))
    step_size = jnp.zeros_like(equivalent)
    for newton_turn in range(NEWTON):
        hardness = harden + step_size
        decay_term = jnp.exp(-RATE * hardness)
        mismatch = equivalent - shear_three * step_size - YIELD - SATURATE * (1.0 - decay_term)
        tangent = shear_three + SATURATE * RATE * decay_term
        active = (newton_turn < costs)[:, None, None]
        step_size = jnp.where(active, step_size + mismatch / tangent, step_size)
    step_size = jnp.where(equivalent > initial_yield, step_size, 0.0)
    shrink = 1.0 - shear_three * step_size / jnp.maximum(equivalent, YIELD)
    stresses = shrink[:, None] * trial_stress
    plastic_new = plastic + (1.0 - shrink)[:, None] * elastic
    harden_new = harden + step_size
    membrane_force = jnp.sum(through[None, None, :, None] * stresses, axis=2)
    moments = jnp.sum((through * heights)[None, None, :, None] * stresses, axis=2)
    shear_modulus = (
        5.0 / 6.0 * jnp.sum(through[None, :, None] * modulus, axis=1) / (2.0 * (1.0 + POISSON))
    )
    shear_force = shear_modulus[:, None, :] * transverse
    weight_x = jnp.array([-0.5, 0.5, 0.5, -0.5], jnp.float32)[None, :, None]
    weight_y = jnp.array([-0.5, -0.5, 0.5, 0.5], jnp.float32)[None, :, None]
    force_u = inverse * (weight_x * membrane_force[:, 0:1] + weight_y * membrane_force[:, 2:3])
    force_v = inverse * (weight_y * membrane_force[:, 1:2] + weight_x * membrane_force[:, 2:3])
    force_w = inverse * (weight_x * shear_force[:, 0:1] + weight_y * shear_force[:, 1:2])
    force_a = (
        inverse * (weight_x * moments[:, 0:1] + weight_y * moments[:, 2:3])
        + 0.25 * shear_force[:, 0:1]
    )
    force_b = (
        inverse * (weight_y * moments[:, 1:2] + weight_x * moments[:, 2:3])
        + 0.25 * shear_force[:, 1:2]
    )
    forces = jnp.stack([force_u, force_v, force_w, force_a, force_b], 1)
    return (forces, plastic_new, harden_new)


def block_tables(nodes, slots, first_nodes, width):
    count = nodes.shape[0]
    corner_nodes = jnp.take_along_axis(nodes, slots.reshape(count, -1), axis=1)
    offsets = corner_nodes - first_nodes[:, None]
    return (jnp.arange(width, dtype=jnp.int32)[None, :, None] == offsets[:, None, :]).astype(
        jnp.float32
    )


def element_forces(windows, tables, state, costs):
    plastic, harden, modulus, inverse = state
    count = tables.shape[0]
    elements = tables.shape[2] // 4
    corner_disp = jnp.einsum("cbw,bwk->cbk", windows, tables, precision=HIGHEST)
    corner_disp = jnp.transpose(corner_disp.reshape(5, count, 4, elements), (1, 0, 2, 3))
    forces, plastic, harden = element_update(corner_disp, inverse, modulus, plastic, harden, costs)
    forces = jnp.transpose(forces, (1, 0, 2, 3)).reshape(5, count, 4 * elements)
    nodal = jnp.einsum("cbk,bwk->cbw", forces, tables, precision=HIGHEST)
    return (nodal, plastic, harden)


def home_windows(extended, stride, count, width):
    pieces = [
        extended[:, q * stride : q * stride + count * stride].reshape(5, count, stride)
        for q in range(width // stride)
    ]
    return jnp.concatenate(pieces, 2)


def home_fold(nodal, stride, count, width):
    total = jnp.zeros((5, count * stride + width), jnp.float32)
    for q in range(width // stride):
        piece = nodal[:, :, q * stride : (q + 1) * stride].reshape(5, count * stride)
        total = total.at[:, q * stride : q * stride + count * stride].add(piece)
    return total


def integrate(disp_now, vel_now, internal, load_now, mass_now, pinned):
    accel = (load_now - internal) / mass_now[None, :]
    vel_now = jnp.where(pinned, 0.0, vel_now + STEP_TIME * accel)
    return (disp_now + STEP_TIME * vel_now, vel_now)


def pack(pick, values):
    return jnp.einsum("sb,b...->s...", pick, values, precision=HIGHEST)


def on_device(
    displacement,
    velocity,
    nodal_load,
    nodal_mass,
    plastic_strain,
    hardening,
    ply_modulus,
    inverse_size,
    cost_map,
    migration_plan,
    block_nodes,
    corner_slot,
):
    group = lax.axis_size("grp")
    member = lax.axis_index("grp")
    station = lax.axis_index("span")
    own_nodes = displacement.shape[2]
    own_blocks = plastic_strain.shape[1]
    window = block_nodes.shape[2]
    stride = own_nodes // own_blocks
    capacity = max(1, (own_blocks + group - 1) // group)
    slots_all = group * capacity
    disp_now = displacement[0]
    vel_now = velocity[0]
    load_now = nodal_load[0]
    mass_now = nodal_mass[0]
    pinned = (station == 0) & (member == 0) & (jnp.arange(own_nodes)[None, :] < window)
    dests = migration_plan[0, :, 0].reshape(group, own_blocks)
    earlier = jnp.arange(own_blocks)[:, None] > jnp.arange(own_blocks)[None, :]
    same = dests[:, :, None] == dests[:, None, :]
    rank = jnp.sum(same & earlier[None], axis=2)
    target = dests * capacity + rank
    my_target = lax.dynamic_index_in_dim(target, member, 0, keepdims=False)
    pick = (jnp.arange(slots_all, dtype=jnp.int32)[:, None] == my_target[None, :]).astype(
        jnp.float32
    )
    first_block = member * own_blocks
    nodes_here = (
        lax.dynamic_slice_in_dim(block_nodes[0], first_block, own_blocks, 0) - member * own_nodes
    )
    slots_here = lax.dynamic_slice_in_dim(corner_slot[0], first_block, own_blocks, 0)
    costs = lax.dynamic_slice_in_dim(cost_map[0], first_block, own_blocks, 0)
    tables = block_tables(
        nodes_here, slots_here, jnp.arange(own_blocks, dtype=jnp.int32) * stride, window
    )
    plastic = plastic_strain[0]
    harden = hardening[0]
    modulus = ply_modulus[0]
    inverse = inverse_size[0]
    for time_step in range(STEPS):
        rim = from_behind(disp_now[:, :window], ("span", "grp"), -1)
        extended = jnp.concatenate([disp_now, rim], 1)
        windows = home_windows(extended, stride, own_blocks, window)
        nodal, plastic, harden = element_forces(
            windows, tables, (plastic, harden, modulus, inverse), costs
        )
        partial_value = home_fold(nodal, stride, own_blocks, window)
        carried = from_behind(partial_value[:, own_nodes:], ("span", "grp"), 1)
        internal = partial_value[:, :own_nodes].at[:, :window].add(carried)
        disp_now, vel_now = integrate(disp_now, vel_now, internal, load_now, mass_now, pinned)
    resident_plastic, resident_hardening = (
        lax.all_to_all(pack(pick, plastic), "grp", split_axis=0, concat_axis=0, tiled=True),
        lax.all_to_all(pack(pick, harden), "grp", split_axis=0, concat_axis=0, tiled=True),
    )
    return (disp_now[None], vel_now[None], resident_plastic[None], resident_hardening[None])


def solution(mesh):
    return jax.shard_map(
        on_device,
        mesh=mesh,
        in_specs=(
            P("span", None, "grp"),
            P("span", None, "grp"),
            P("span", None, "grp"),
            P("span", "grp"),
            P("span", "grp", None, None, None),
            P("span", "grp", None, None),
            P("span", "grp", None, None),
            P("span", "grp", None),
            P("span", None),
            P("span", None, None),
            P("span", None, None),
            P("span", None, None, None),
        ),
        out_specs=(
            P("span", None, "grp"),
            P("span", None, "grp"),
            P("span", "grp", None, None, None),
            P("span", "grp", None, None),
        ),
        check_vma=False,
    )
```

profile of v0, /device:TPU:193, one launch (start us, length us, event | category | flops | bytes accessed | tf_op | source)
XLA Modules:
  0.0 210.1 jit_solution(1130510538347841655)
XLA Ops:
  0.6 0.8 copy.408
  1.5 7.9 %collective-permute-start = (f32[5,256]{1,0:T(8,128)S(1)}, f32[5,256]{1,0:T(8,128)S(1)}, u32[]{:S(2)}, u32[]{:S(2)}) collective-permute-start(f32[5,256]{1,0:T(8,128)S(1)} %slice.1006), channel_id=1, source_target_pairs={{1,0},{2,1},{3,2},{4,3},{5,4},{6,5},{7,6},{8,7},{9,8},{10,9},{11,1... | collective-permute-start | bytes 15368 | tf_op jit(solution)/shard_map/ppermute | solution.py:21
  9.4 0.7 broadcast_multiply_fusion.1
  10.1 0.9 fusion.124
  10.9 0.7 compare_bitcast_fusion.3
  11.7 0.7 subtract_bitcast_fusion.4
  12.5 65.0 %gather_fusion = s32[8192]{0:T(1024)S(1)} fusion(s32[16,256]{1,0:T(8,128)S(1)} %subtract_bitcast_fusion.4, s32[8192]{0:T(1024)S(1)} %bitcast.964), kind=kCustom, calls=%fused_computation | custom fusion | bytes 131072 | tf_op jit(solution)/shard_map/jit(take_along_axis)/gather | solution.py:94
  77.7 0.6 compare_reduce_fusion.4
  78.4 0.6 compare_reduce_fusion.3
  79.0 0.6 compare_reduce_fusion.2
  79.6 0.7 compare_reduce_fusion.1
  80.7 2.7 %fusion.16 = f32[5,16,512]{2,0,1:T(8,128)S(1)} fusion(s32[16,512]{1,0:T(8,128)S(1)} %select_subtract_fusion, f32[5,16,64]{2,0,1:T(8,128)S(1)} %copy.252, f32[5,16,64]{2,0,1:T(8,128)S(1)} %copy.251, f32[5,16,64]{2,0,1:T(8,128)S(1)} %copy.250, f32[5,16,64]{2,0,1:T(8,128)S(1)} %copy.249), kind=kOutput, calls=%fused_computation.18 | convolution fusion | flops 127987712 | bytes 278528 | tf_op jit(solution)/shard_map/cbw,bwk->cbk/dot_general | solution.py:105
  85.4 3.8 %fusion.20 = f32[5,16,256]{2,0,1:T(8,128)S(1)} fusion(s32[16,512]{1,0:T(8,128)S(1)} %select_subtract_fusion, f32[5,16,512]{2,1,0:T(8,128)S(1)} %reshape.1161), kind=kOutput, calls=%fused_computation.22 | convolution fusion | flops 127926272 | bytes 278528 | tf_op jit(solution)/shard_map/cbk,bwk->cbw/dot_general | solution.py:109
  89.2 0.8 fusion.511
  90.3 0.7 add_select_fusion.35
  91.6 0.7 fusion.426
  92.2 0.8 add_select_fusion.33
  93.5 1.9 collective-permute-start.1
  95.4 0.6 compare_reduce_fusion
  96.1 5.7 %collective-permute-done.1 = f32[5,256]{1,0:T(8,128)S(1)} collective-permute-done((f32[5,256]{1,0:T(8,128)S(1)}, f32[5,256]{1,0:T(8,128)S(1)}, u32[]{:S(2)}, u32[]{:S(2)}) %collective-permute-start.1) | collective-permute-done | bytes 5152 | tf_op jit(solution)/shard_map/ppermute | solution.py:21
  101.8 0.6 fusion.468
  102.4 2.1 %collective-permute-start.2 = (f32[5,256]{1,0:T(8,128)S(1)}, f32[5,256]{1,0:T(8,128)S(1)}, u32[]{:S(2)}, u32[]{:S(2)}) collective-permute-start(f32[5,256]{1,0:T(8,128)S(1)} %slice.1047), channel_id=1, source_target_pairs={{1,0},{2,1},{3,2},{4,3},{5,4},{6,5},{7,6},{8,7},{9,8},{10,9},{11,1... | collective-permute-start | bytes 15368 | tf_op jit(solution)/shard_map/ppermute | solution.py:21
  104.7 2.2 %collective-permute-done.2 = f32[5,256]{1,0:T(8,128)S(1)} collective-permute-done((f32[5,256]{1,0:T(8,128)S(1)}, f32[5,256]{1,0:T(8,128)S(1)}, u32[]{:S(2)}, u32[]{:S(2)}) %collective-permute-start.2) | collective-permute-done | bytes 5152 | tf_op jit(solution)/shard_map/ppermute | solution.py:21
  107.2 2.7 %fusion.17 = f32[5,16,512]{2,0,1:T(8,128)S(1)} fusion(s32[16,512]{1,0:T(8,128)S(1)} %select_subtract_fusion, f32[5,16,64]{2,0,1:T(8,128)S(1)} %copy.264, f32[5,16,64]{2,0,1:T(8,128)S(1)} %copy.263, f32[5,16,64]{2,0,1:T(8,128)S(1)} %copy.262, f32[5,16,64]{2,0,1:T(8,128)S(1)} %copy.261), kind=kOutput, calls=%fused_computation.19 | convolution fusion | flops 127987712 | bytes 278528 | tf_op jit(solution)/shard_map/cbw,bwk->cbk/dot_general | solution.py:105
  111.1 3.8 %fusion.21 = f32[5,16,256]{2,0,1:T(8,128)S(1)} fusion(s32[16,512]{1,0:T(8,128)S(1)} %select_subtract_fusion, f32[5,16,512]{2,1,0:T(8,128)S(1)} %reshape.1171), kind=kOutput, calls=%fused_computation.23 | convolution fusion | flops 127926272 | bytes 278528 | tf_op jit(solution)/shard_map/cbk,bwk->cbw/dot_general | solution.py:109
  114.9 0.8 fusion.510
  116.1 0.7 add_select_fusion.32
  117.3 0.7 fusion.427
  117.9 0.8 add_select_fusion.30
  119.2 1.9 collective-permute-start.3
  121.1 6.3 %collective-permute-done.3 = f32[5,256]{1,0:T(8,128)S(1)} collective-permute-done((f32[5,256]{1,0:T(8,128)S(1)}, f32[5,256]{1,0:T(8,128)S(1)}, u32[]{:S(2)}, u32[]{:S(2)}) %collective-permute-start.3) | collective-permute-done | bytes 5152 | tf_op jit(solution)/shard_map/ppermute | solution.py:21
  127.5 0.6 fusion.469
  128.1 3.4 %collective-permute-start.4 = (f32[5,256]{1,0:T(8,128)S(1)}, f32[5,256]{1,0:T(8,128)S(1)}, u32[]{:S(2)}, u32[]{:S(2)}) collective-permute-start(f32[5,256]{1,0:T(8,128)S(1)} %slice.1088), channel_id=1, source_target_pairs={{1,0},{2,1},{3,2},{4,3},{5,4},{6,5},{7,6},{8,7},{9,8},{10,9},{11,1... | collective-permute-start | bytes 15368 | tf_op jit(solution)/shard_map/ppermute | solution.py:21
  131.6 0.9 collective-permute-done.4
  132.9 2.7 %fusion.18 = f32[5,16,512]{2,0,1:T(8,128)S(1)} fusion(s32[16,512]{1,0:T(8,128)S(1)} %select_subtract_fusion, f32[5,16,64]{2,0,1:T(8,128)S(1)} %copy.275, f32[5,16,64]{2,0,1:T(8,128)S(1)} %copy.274, f32[5,16,64]{2,0,1:T(8,128)S(1)} %copy.273, f32[5,16,64]{2,0,1:T(8,128)S(1)} %copy.272), kind=kOutput, calls=%fused_computation.20 | convolution fusion | flops 127987712 | bytes 278528 | tf_op jit(solution)/shard_map/cbw,bwk->cbk/dot_general | solution.py:105
  136.8 3.8 %fusion.22 = f32[5,16,256]{2,0,1:T(8,128)S(1)} fusion(s32[16,512]{1,0:T(8,128)S(1)} %select_subtract_fusion, f32[5,16,512]{2,1,0:T(8,128)S(1)} %reshape.1181), kind=kOutput, calls=%fused_computation.24 | convolution fusion | flops 127926272 | bytes 278528 | tf_op jit(solution)/shard_map/cbk,bwk->cbw/dot_general | solution.py:109
  140.6 0.8 fusion.509
  141.8 0.7 add_select_fusion.29
  143.0 0.7 fusion.428
  143.7 0.8 add_select_fusion.27
  144.9 1.9 collective-permute-start.5
  146.8 0.5 broadcast.2348
  147.4 0.7 reduce.76
  148.2 5.1 %collective-permute-done.5 = f32[5,256]{1,0:T(8,128)S(1)} collective-permute-done((f32[5,256]{1,0:T(8,128)S(1)}, f32[5,256]{1,0:T(8,128)S(1)}, u32[]{:S(2)}, u32[]{:S(2)}) %collective-permute-start.5) | collective-permute-done | bytes 5152 | tf_op jit(solution)/shard_map/ppermute | solution.py:21
  153.3 0.6 fusion.470
  153.9 4.2 %collective-permute-start.6 = (f32[5,256]{1,0:T(8,128)S(1)}, f32[5,256]{1,0:T(8,128)S(1)}, u32[]{:S(2)}, u32[]{:S(2)}) collective-permute-start(f32[5,256]{1,0:T(8,128)S(1)} %slice.1129), channel_id=1, source_target_pairs={{1,0},{2,1},{3,2},{4,3},{5,4},{6,5},{7,6},{8,7},{9,8},{10,9},{11,1... | collective-permute-start | bytes 15368 | tf_op jit(solution)/shard_map/ppermute | solution.py:21
  159.3 2.7 %fusion.19 = f32[5,16,512]{2,0,1:T(8,128)S(1)} fusion(s32[16,512]{1,0:T(8,128)S(1)} %select_subtract_fusion, f32[5,16,64]{2,0,1:T(8,128)S(1)} %copy.286, f32[5,16,64]{2,0,1:T(8,128)S(1)} %copy.285, f32[5,16,64]{2,0,1:T(8,128)S(1)} %copy.284, f32[5,16,64]{2,0,1:T(8,128)S(1)} %copy.283), kind=kOutput, calls=%fused_computation.21 | convolution fusion | flops 127987712 | bytes 278528 | tf_op jit(solution)/shard_map/cbw,bwk->cbk/dot_general | solution.py:105
  162.4 0.9 fusion.75
  163.3 0.7 copy.298
  164.0 15.4 %all-to-all-start.1 = ((f32[32,5,128]{2,1,0:T(8,128)}), f32[32,5,128]{2,1,0:T(8,128)S(1)}, u32[]{:S(2)}, u32[]{:S(2)}) async-start(f32[32,5,128]{2,1,0:T(8,128)} %copy.298), calls=%async_computation.1 | async-start | bytes 262144 | tf_op jit(solution)/shard_map/all_to_all | solution.py:202
  180.1 0.9 copy.297
  181.5 3.8 %fusion.23 = f32[5,16,256]{2,0,1:T(8,128)S(1)} fusion(s32[16,512]{1,0:T(8,128)S(1)} %select_subtract_fusion, f32[5,16,512]{2,1,0:T(8,128)S(1)} %reshape.1191), kind=kOutput, calls=%fused_computation.25 | convolution fusion | flops 127926272 | bytes 278528 | tf_op jit(solution)/shard_map/cbk,bwk->cbw/dot_general | solution.py:109
  185.3 0.8 fusion.508
  186.4 0.7 add_select_fusion.26
  187.6 0.7 fusion.429
  188.4 8.9 %all-to-all-start = ((f32[32,3,5,128]{3,1,2,0:T(4,128)}), f32[32,3,5,128]{3,1,2,0:T(4,128)S(1)}, u32[]{:S(2)}, u32[]{:S(2)}) async-start(f32[32,3,5,128]{3,1,2,0:T(4,128)} %copy.297), calls=%async_computation | async-start | bytes 655360 | tf_op jit(solution)/shard_map/all_to_all | solution.py:201
  197.3 0.8 add_select_fusion.24
  198.6 3.1 %collective-permute-start.7 = (f32[5,256]{1,0:T(8,128)S(1)}, f32[5,256]{1,0:T(8,128)S(1)}, u32[]{:S(2)}, u32[]{:S(2)}) collective-permute-start(f32[5,256]{1,0:T(8,128)S(1)} %slice.1169), channel_id=1, source_target_pairs={{0,1},{1,2},{2,3},{3,4},{4,5},{5,6},{6,7},{7,8},{8,9},{9,10},{10,1... | collective-permute-start | bytes 15368 | tf_op jit(solution)/shard_map/ppermute | solution.py:21
  201.7 5.2 %collective-permute-done.7 = f32[5,256]{1,0:T(8,128)S(1)} collective-permute-done((f32[5,256]{1,0:T(8,128)S(1)}, f32[5,256]{1,0:T(8,128)S(1)}, u32[]{:S(2)}, u32[]{:S(2)}) %collective-permute-start.7) | collective-permute-done | bytes 5152 | tf_op jit(solution)/shard_map/ppermute | solution.py:21
  206.9 0.6 fusion.471
  207.5 0.6 copy.299
  208.1 0.6 copy.300
  208.8 0.7 copy.302
  209.4 0.7 copy.301
  (224 shorter events, 13.8 us)
Async XLA Ops:
  0.6 11.0 %copy-start = (s32[1,512,4,128]{3,2,1,0:T(4,128)S(1)}, s32[1,512,4,128]{3,2,1,0:T(4,128)}, u32[]{:S(2)}) copy-start(s32[1,512,4,128]{3,2,1,0:T(4,128)} %param.79) | copy-start | bytes 3145732
  1.5 78.9 %collective-permute-start = (f32[5,256]{1,0:T(8,128)S(1)}, f32[5,256]{1,0:T(8,128)S(1)}, u32[]{:S(2)}, u32[]{:S(2)}) collective-permute-start(f32[5,256]{1,0:T(8,128)S(1)} %slice.1006), channel_id=1, source_target_pairs={{1,0},{2,1},{3,2},{4,3},{5,4},{6,5},{7,6},{8,7},{9,8},{10,9},{11,1... | collective-permute-start | bytes 15368 | tf_op jit(solution)/shard_map/ppermute | solution.py:21
  12.5 65.1 %copy-start.8 = (f32[1,5,1024]{2,0,1:T(1,128)S(1)}, f32[1,5,1024]{2,0,1:T(1,128)}, u32[]{:S(2)}) copy-start(f32[1,5,1024]{2,0,1:T(1,128)} %param.68) | copy-start | bytes 61444
  83.5 0.9 copy-start.2
  83.5 0.9 copy-start.11
  83.5 1.0 copy-start.3
  83.5 1.0 copy-start.4
  83.6 1.1 copy-start.12
  83.6 1.1 copy-start.13
  83.6 1.2 copy-start.1
  83.6 1.2 copy-start.6
  83.7 1.2 copy-start.7
  89.2 13.2 %copy-start.5 = (f32[1,5,1024]{2,0,1:T(1,128)S(1)}, f32[1,5,1024]{2,0,1:T(1,128)}, u32[]{:S(2)}) copy-start(f32[1,5,1024]{2,0,1:T(1,128)} %param.70) | copy-start | bytes 61444
  89.2 13.2 %copy-start.9 = (f32[1,5,1024]{2,0,1:T(1,128)S(1)}, f32[1,5,1024]{2,0,1:T(1,128)}, u32[]{:S(2)}) copy-start(f32[1,5,1024]{2,0,1:T(1,128)} %param.69) | copy-start | bytes 61444
  89.2 13.2 %copy-start.10 = (f32[1,1024]{1,0:T(1,128)S(1)}, f32[1,1024]{1,0:T(1,128)}, u32[]{:S(2)}) copy-start(f32[1,1024]{1,0:T(1,128)} %param.71) | copy-start | bytes 12292
  93.5 8.3 %collective-permute-start.1 = (f32[5,256]{1,0:T(8,128)S(1)}, f32[5,256]{1,0:T(8,128)S(1)}, u32[]{:S(2)}, u32[]{:S(2)}) collective-permute-start(f32[5,256]{1,0:T(8,128)S(1)} %slice.1046), channel_id=1, source_target_pairs={{0,1},{1,2},{2,3},{3,4},{4,5},{5,6},{6,7},{7,8},{8,9},{9,10},{10,1... | collective-permute-start | bytes 15368 | tf_op jit(solution)/shard_map/ppermute | solution.py:21
  102.4 4.4 %collective-permute-start.2 = (f32[5,256]{1,0:T(8,128)S(1)}, f32[5,256]{1,0:T(8,128)S(1)}, u32[]{:S(2)}, u32[]{:S(2)}) collective-permute-start(f32[5,256]{1,0:T(8,128)S(1)} %slice.1047), channel_id=1, source_target_pairs={{1,0},{2,1},{3,2},{4,3},{5,4},{6,5},{7,6},{8,7},{9,8},{10,9},{11,1... | collective-permute-start | bytes 15368 | tf_op jit(solution)/shard_map/ppermute | solution.py:21
  119.2 8.3 %collective-permute-start.3 = (f32[5,256]{1,0:T(8,128)S(1)}, f32[5,256]{1,0:T(8,128)S(1)}, u32[]{:S(2)}, u32[]{:S(2)}) collective-permute-start(f32[5,256]{1,0:T(8,128)S(1)} %slice.1087), channel_id=1, source_target_pairs={{0,1},{1,2},{2,3},{3,4},{4,5},{5,6},{6,7},{7,8},{8,9},{9,10},{10,1... | collective-permute-start | bytes 15368 | tf_op jit(solution)/shard_map/ppermute | solution.py:21
  128.1 4.4 %collective-permute-start.4 = (f32[5,256]{1,0:T(8,128)S(1)}, f32[5,256]{1,0:T(8,128)S(1)}, u32[]{:S(2)}, u32[]{:S(2)}) collective-permute-start(f32[5,256]{1,0:T(8,128)S(1)} %slice.1088), channel_id=1, source_target_pairs={{1,0},{2,1},{3,2},{4,3},{5,4},{6,5},{7,6},{8,7},{9,8},{10,9},{11,1... | collective-permute-start | bytes 15368 | tf_op jit(solution)/shard_map/ppermute | solution.py:21
  140.6 6.8 %copy-start.14 = (s32[1,512,1]{1,2,0:T(1,128)S(1)}, s32[1,512,1]{1,2,0:T(1,128)}, u32[]{:S(2)}) copy-start(s32[1,512,1]{1,2,0:T(1,128)} %param.77) | copy-start | bytes 6148
  144.9 8.4 %collective-permute-start.5 = (f32[5,256]{1,0:T(8,128)S(1)}, f32[5,256]{1,0:T(8,128)S(1)}, u32[]{:S(2)}, u32[]{:S(2)}) collective-permute-start(f32[5,256]{1,0:T(8,128)S(1)} %slice.1128), channel_id=1, source_target_pairs={{0,1},{1,2},{2,3},{3,4},{4,5},{5,6},{6,7},{7,8},{8,9},{9,10},{10,1... | collective-permute-start | bytes 15368 | tf_op jit(solution)/shard_map/ppermute | solution.py:21
  153.9 5.0 %collective-permute-start.6 = (f32[5,256]{1,0:T(8,128)S(1)}, f32[5,256]{1,0:T(8,128)S(1)}, u32[]{:S(2)}, u32[]{:S(2)}) collective-permute-start(f32[5,256]{1,0:T(8,128)S(1)} %slice.1129), channel_id=1, source_target_pairs={{1,0},{2,1},{3,2},{4,3},{5,4},{6,5},{7,6},{8,7},{9,8},{10,9},{11,1... | collective-permute-start | bytes 15368 | tf_op jit(solution)/shard_map/ppermute | solution.py:21
  164.0 24.5 %all-to-all-start.1 = ((f32[32,5,128]{2,1,0:T(8,128)}), f32[32,5,128]{2,1,0:T(8,128)S(1)}, u32[]{:S(2)}, u32[]{:S(2)}) async-start(f32[32,5,128]{2,1,0:T(8,128)} %copy.298), calls=%async_computation.1 | async-start | bytes 262144 | tf_op jit(solution)/shard_map/all_to_all | solution.py:202
  188.4 21.0 %all-to-all-start = ((f32[32,3,5,128]{3,1,2,0:T(4,128)}), f32[32,3,5,128]{3,1,2,0:T(4,128)S(1)}, u32[]{:S(2)}, u32[]{:S(2)}) async-start(f32[32,3,5,128]{3,1,2,0:T(4,128)} %copy.297), calls=%async_computation | async-start | bytes 655360 | tf_op jit(solution)/shard_map/all_to_all | solution.py:201
  198.6 8.3 %collective-permute-start.7 = (f32[5,256]{1,0:T(8,128)S(1)}, f32[5,256]{1,0:T(8,128)S(1)}, u32[]{:S(2)}, u32[]{:S(2)}) collective-permute-start(f32[5,256]{1,0:T(8,128)S(1)} %slice.1169), channel_id=1, source_target_pairs={{0,1},{1,2},{2,3},{3,4},{4,5},{5,6},{6,7},{7,8},{8,9},{9,10},{10,1... | collective-permute-start | bytes 15368 | tf_op jit(solution)/shard_map/ppermute | solution.py:21
where the time goes:
time: 211 us; the launch traced here: 210 us
  local copies, waits for them, and re-layouts  79.1 us (37%)
  starting transfers between devices  50.7 us (24%)
  matrix products  27.4 us (13%)
  waiting for transfers between devices  25.9 us (12%)
  other arithmetic  25.3 us (12%)
    gather x2, local copies, waits for them, and re-layouts, block_tables(): corner_nodes = jnp.take_along_axis(nodes, slots.reshape(count, -1), axis=1)  65 us
    ppermute x8, starting transfers between devices, from_behind(): return lax.ppermute(shard, axis, pairs)  26.5 us
    ppermute x8, waiting for transfers between devices, from_behind(): return lax.ppermute(shard, axis, pairs)  25.8 us
    all_to_all x1, starting transfers between devices, on_device(): lax.all_to_all(pack(pick, harden), 'grp', split_axis=0, concat_axis=0, ti...  15.4 us
    dot_general x4, matrix products, element_forces(): nodal = jnp.einsum('cbk,bwk->cbw', forces, tables, precision=HIGHEST)  15.3 us
    dot_general x4, matrix products, element_forces(): corner_disp = jnp.einsum('cbw,bwk->cbk', windows, tables, precision=HIGHEST)  10.9 us
    another operation x13, other arithmetic  9.15 us
    all_to_all x1, starting transfers between devices, on_device(): lax.all_to_all(pack(pick, plastic), 'grp', split_axis=0, concat_axis=0, t...  8.86 us
  transfers between devices with their start and end apart: 10, of which 8 were waited for; matrix products, arithmetic and copies ran while one was open for 41% of the time, Pallas kernels for 0%

commit v1 on v0

v1 whole, which is shorter than its diff:
```python
import jax
import jax.numpy as jnp
from jax import lax
from jax.experimental import pallas as pl
from jax.experimental.pallas import tpu as pltpu
from jax.sharding import PartitionSpec as P

NEWTON = 4
STEPS = 4
POISSON = 0.3
YIELD = 0.1
SATURATE = 0.1
RATE = 20.0
STEP_TIME = 0.25
HEIGHTS = (-0.5, -0.25, 0.0, 0.25, 0.5)
THROUGH = (1.0 / 12, 4.0 / 12, 2.0 / 12, 4.0 / 12, 1.0 / 12)

OWN = 16
LEFT = 12
RIGHT = 9
BLOCKS = LEFT + OWN + RIGHT
ROWS = 40
NROW = 20
NPAD = 24
COMP = 31
PL_ROWS = 472
PR_ROWS = 376
C_H, C_M, C_Z, C_I, C_C = 15, 20, 25, 26, 30
F32 = jnp.float32
BF16 = jnp.bfloat16


def shift(shard, by):
    size = lax.axis_size(("span", "grp"))
    pairs = [(i, i + by) for i in range(size) if 0 <= i + by < size]
    return lax.ppermute(shard, ("span", "grp"), pairs)


def lanes(values, index):
    return jnp.take_along_axis(values, index, axis=1)


def pack_kernel(cost, nodes, slots, pst, hrd, mod, inv, dis, vel, load, mass, to_right, to_left, own):
    first = lax.axis_index("grp") * OWN
    for j in range(OWN):
        own[4, j : j + 1, :] = jnp.full((1, 128), cost[first + j], jnp.int32).astype(F32)
    for o in range(2):
        rows = slice(8 * o, 8 * o + 8)
        low, high = nodes[rows, 0:128], nodes[rows, 128:256]
        base = (first + 8 * o + lax.broadcasted_iota(jnp.int32, (8, 128), 0)) * 64
        for k in range(4):
            slot = slots[rows, k, :]
            lane = slot & 127
            node = jnp.where(slot < 128, lanes(low, lane), lanes(high, lane))
            own[k, rows, :] = (node - base).astype(F32)

    def rows_of(c, at, count):
        if c < 15:
            return pst[c // 5, c % 5, at : at + count, :]
        if c < 20:
            return hrd[c - 15, at : at + count, :]
        if c < 25:
            return mod[c - 20, at : at + count, :]
        if c == 25:
            return inv[at : at + count, :]
        return own[c - 26, at : at + count, :]

    for c in range(COMP):
        to_right[c * LEFT : (c + 1) * LEFT, :] = rows_of(c, OWN - LEFT, LEFT)
        to_left[c * RIGHT : (c + 1) * RIGHT, :] = rows_of(c, 0, RIGHT)
    for i in range(16):
        source = (dis, vel, load)[i // 5] if i < 15 else mass
        values = source[i % 5] if i < 15 else source[...]
        to_right[COMP * LEFT + 6 * i : COMP * LEFT + 6 * i + 6, :] = values[2:8]
        to_left[COMP * RIGHT + 6 * i : COMP * RIGHT + 6 * i + 6, :] = values[0:6]


def element_octet(disp, state, consts, costs, inv):
    half = 0.5 * inv
    dx = [half * (u[1] + u[2] - u[0] - u[3]) for u in disp]
    dy = [half * (u[2] + u[3] - u[0] - u[1]) for u in disp]
    mean_a = 0.25 * (disp[3][0] + disp[3][1] + disp[3][2] + disp[3][3])
    mean_b = 0.25 * (disp[4][0] + disp[4][1] + disp[4][2] + disp[4][3])
    membrane = (dx[0], dy[1], dy[0] + dx[1])
    bending = (dx[3], dy[4], dy[3] + dx[4])
    shear = (dx[2] + mean_a, dy[2] + mean_b)
    active = [costs > float(t) for t in range(NEWTON)]
    new_state = []
    force = [None] * 3
    moment = [None] * 3
    modulus_sum = None
    for p in range(5):
        plastic, harden, modulus = state[p]
        elastic = [membrane[i] + HEIGHTS[p] * bending[i] - plastic[i] for i in range(3)]
        stiff = modulus * (1.0 / (1.0 - POISSON * POISSON))
        t0 = stiff * (elastic[0] + POISSON * elastic[1])
        t1 = stiff * (POISSON * elastic[0] + elastic[1])
        t2 = stiff * (0.5 * (1.0 - POISSON)) * elastic[2]
        s0 = t0 - 0.5 * t1
        q = jnp.sqrt(s0 * s0 + 0.75 * (t1 * t1) + 3.0 * (t2 * t2))
        g3 = modulus * (1.5 / (1.0 + POISSON))
        decay = jnp.exp(-RATE * harden)
        above = q - YIELD - SATURATE * (1.0 - decay)
        plastic_flow = above > 0.0
        step = above / (g3 + SATURATE * RATE * decay)
        for turn in range(1, NEWTON):
            decay = jnp.exp(-RATE * (harden + step))
            miss = q - g3 * step - YIELD - SATURATE * (1.0 - decay)
            step = jnp.where(active[turn], step + miss / (g3 + SATURATE * RATE * decay), step)
        step = jnp.where(plastic_flow, step, 0.0)
        loss = g3 * step / jnp.maximum(q, YIELD)
        keep = 1.0 - loss
        stress = (keep * t0, keep * t1, keep * t2)
        new_state.append(([plastic[i] + loss * elastic[i] for i in range(3)], harden + step))
        for i in range(3):
            part = THROUGH[p] * stress[i]
            force[i] = part if force[i] is None else force[i] + part
            if HEIGHTS[p] != 0.0:
                part = THROUGH[p] * HEIGHTS[p] * stress[i]
                moment[i] = part if moment[i] is None else moment[i] + part
        part = THROUGH[p] * modulus
        modulus_sum = part if modulus_sum is None else modulus_sum + part
    shear_modulus = modulus_sum * (5.0 / 6.0 / (2.0 * (1.0 + POISSON)))
    q0, q1 = shear_modulus * shear[0], shear_modulus * shear[1]
    n = [half * f for f in force]
    m = [half * f for f in moment]
    along_x = (n[0], n[2], half * q0, m[0], m[2])
    along_y = (n[2], n[1], half * q1, m[2], m[1])
    even = (None, None, None, 0.25 * q0, 0.25 * q1)
    return new_state, (along_x, along_y, even)


def step_kernel(
    plan, halo_l, halo_r, own, pst, hrd, mod, inv, dis, vel, load, mass,
    dis_out, vel_out, send,
    st, nd, rm, tab, win, grp, acc, itn,
):
    for c in range(COMP):
        if c < 15:
            mine = pst[c // 5, c % 5]
        elif c < 20:
            mine = hrd[c - 15]
        elif c < 25:
            mine = mod[c - 20]
        elif c == 25:
            mine = inv[...]
        else:
            mine = own[c - 26]
        at = c * ROWS
        st[at : at + LEFT, :] = halo_l[c * LEFT : (c + 1) * LEFT, :]
        st[at + LEFT : at + LEFT + OWN, :] = mine
        st[at + LEFT + OWN : at + BLOCKS, :] = halo_r[c * RIGHT : (c + 1) * RIGHT, :]
        st[at + BLOCKS : at + ROWS, :] = jnp.zeros((ROWS - BLOCKS, 128), F32)
    pinned = (lax.axis_index("span") == 0) & (lax.axis_index("grp") == 0)
    free_rows = jnp.where(
        pinned & (lax.broadcasted_iota(jnp.int32, (8, 128), 0) < 2), 0.0, 1.0
    ).astype(F32)
    for i in range(16):
        left = halo_l[COMP * LEFT + 6 * i : COMP * LEFT + 6 * i + 6, :]
        right = halo_r[COMP * RIGHT + 6 * i : COMP * RIGHT + 6 * i + 6, :]
        if i < 15:
            mine = (dis, vel, load)[i // 5][i % 5]
            if 5 <= i < 10:
                mine = mine * free_rows
            nd[i, 0:6, :] = left
            nd[i, 6:14, :] = mine
            nd[i, 14:20, :] = right
            nd[i, 20:32, :] = jnp.zeros((12, 128), F32)
        else:
            rm[0:6, :] = left
            rm[6:14, :] = mass[...]
            rm[14:20, :] = right
            rm[20:24, :] = jnp.zeros((4, 128), F32)
    weight = rm[...]
    there = weight > 0.0
    weight = jnp.where(there, STEP_TIME / jnp.where(there, weight, 1.0), 0.0)
    rm[...] = weight
    rm[6:14, :] = rm[6:14, :] * free_rows
    grp[...] = jnp.zeros(grp.shape, F32)

    def build(b, _):
        spot = lax.broadcasted_iota(jnp.int32, (256, 128), 0).astype(F32).astype(BF16)
        one, zero = jnp.ones((), BF16), jnp.zeros((), BF16)
        hit = []
        for k in range(4):
            row = st[pl.ds((C_I + k) * ROWS + b, 1), :].astype(BF16)
            hit.append(jnp.where(spot == row, one, zero))
        p, q = hit[1] - hit[3], hit[2] - hit[0]
        tab[b, :, 0:128] = p + q
        tab[b, :, 128:256] = q - p
        tab[b, :, 256:384] = (hit[1] + hit[3]) + (hit[0] + hit[2])
        return 0

    lax.fori_loop(0, ROWS, build, 0)

    lane = lax.broadcasted_iota(jnp.int32, (NPAD, 128), 1)

    def time_step(t, _):
        acc[...] = jnp.zeros(acc.shape, F32)
        for d in range(5):
            here = nd[d, 0:NPAD, :]
            rolled = pltpu.roll(here, 64, 1)
            after = pltpu.roll(nd[d, 1 : NPAD + 1, :], 64, 1)
            win[d, pl.ds(0, NPAD, stride=2), :] = here
            win[d, pl.ds(1, NPAD, stride=2), :] = jnp.where(lane < 64, rolled, after)

        def octet(o, _):
            at = pl.multiple_of(o * 8, 8)

            def comp(c):
                return st[pl.ds(pl.multiple_of(c * ROWS + at, 8), 8), :]

            index = [comp(C_I + k).astype(jnp.int32) for k in range(4)]
            near = [i < 128 for i in index]
            spot = [i & 127 for i in index]
            disp = []
            for d in range(5):
                low = win[d, pl.ds(at, 8), :]
                high = win[d, pl.ds(at + 2, 8), :]
                disp.append([jnp.where(near[k], lanes(low, spot[k]), lanes(high, spot[k])) for k in range(4)])
            state = [([comp(i * 5 + p) for i in range(3)], comp(C_H + p), comp(C_M + p)) for p in range(5)]
            new_state, parts = element_octet(disp, state, None, comp(C_C), comp(C_Z))
            for p in range(5):
                plastic, harden = new_state[p]
                for i in range(3):
                    st[pl.ds(pl.multiple_of((i * 5 + p) * ROWS + at, 8), 8), :] = plastic[i]
                st[pl.ds(pl.multiple_of((C_H + p) * ROWS + at, 8), 8), :] = harden
            for s in range(3):
                for d in range(5):
                    if parts[s][d] is not None:
                        grp[s, pl.ds(d, 8, stride=8), :] = parts[s][d]
            totals = [[None] * 5, [None] * 5]
            for j in range(8):
                values = jnp.concatenate([grp[s, 8 * j : 8 * j + 8, :] for s in range(3)], axis=1)
                high = values.astype(BF16)
                low = (values - high.astype(F32)).astype(BF16)
                both = jnp.concatenate([high, low], axis=0)
                out = lax.dot_general(
                    both, tab[at + j], (((1,), (1,)), ((), ())), preferred_element_type=F32
                )
                out = out[0:8] + out[8:16]
                row = totals[j % 2]
                for h in range(2):
                    piece = out[:, 128 * h : 128 * h + 128]
                    r = j // 2 + h
                    row[r] = piece if row[r] is None else row[r] + piece
            for par in range(2):
                for r in range(5):
                    acc[par, o * 4 + r] = acc[par, o * 4 + r] + totals[par][r]
            return 0

        low_octet = jnp.where(t >= 3, 1, 0)
        high_octet = jnp.where(t >= 2, 4, 5)
        lax.fori_loop(low_octet, high_octet, octet, 0)
        half = lax.broadcasted_iota(jnp.int32, (8, 128), 1) < 64
        before = jnp.zeros((8, 128), F32)
        for r in range(NROW):
            odd = pltpu.roll(acc[1, r], 64, 1)
            itn[pl.ds(r, 8, stride=NPAD), :] = acc[0, r] + jnp.where(half, before, odd)
            before = odd
        weight = rm[...]
        for d in range(5):
            speed = nd[5 + d, 0:NPAD, :] + weight * (nd[10 + d, 0:NPAD, :] - itn[d * NPAD : (d + 1) * NPAD, :])
            nd[5 + d, 0:NPAD, :] = speed
            nd[d, 0:NPAD, :] = nd[d, 0:NPAD, :] + STEP_TIME * speed
        return 0

    itn[...] = jnp.zeros(itn.shape, F32)
    lax.fori_loop(0, STEPS, time_step, 0)
    for d in range(5):
        dis_out[d] = nd[d, 6:14, :]
        vel_out[d] = nd[5 + d, 6:14, :]
    send[...] = jnp.zeros(send.shape, F32)
    first = lax.axis_index("grp") * OWN
    for j in range(OWN):
        send[plan[first + j]] = st[pl.ds(LEFT + j, 20, stride=ROWS), :]


def unpack_kernel(recv, pst, hrd):
    for c in range(20):
        for o in range(4):
            values = recv[8 * o : 8 * o + 8, c, :]
            if c < 15:
                pst[c // 5, c % 5, 8 * o : 8 * o + 8, :] = values
            else:
                hrd[c - 15, 8 * o : 8 * o + 8, :] = values


def vmem(count):
    return [pl.BlockSpec(memory_space=pltpu.VMEM) for _ in range(count)]


def on_device(
    displacement,
    velocity,
    nodal_load,
    nodal_mass,
    plastic_strain,
    hardening,
    ply_modulus,
    inverse_size,
    cost_map,
    migration_plan,
    block_nodes,
    corner_slot,
):
    member = lax.axis_index("grp")
    dis = displacement.reshape(5, 8, 128)
    vel = velocity.reshape(5, 8, 128)
    load = nodal_load.reshape(5, 8, 128)
    mass = nodal_mass.reshape(8, 128)
    pst = jnp.transpose(plastic_strain[0], (1, 2, 0, 3))
    hrd = jnp.transpose(hardening[0], (1, 0, 2))
    mod = jnp.transpose(ply_modulus[0], (1, 0, 2))
    inv = inverse_size[0]
    nodes = lax.dynamic_slice_in_dim(block_nodes[0], member * OWN, OWN, 0)
    slots = lax.dynamic_slice_in_dim(corner_slot[0], member * OWN, OWN, 0)
    smem = pl.BlockSpec(memory_space=pltpu.SMEM)
    to_right, to_left, own = pl.pallas_call(
        pack_kernel,
        out_shape=(
            jax.ShapeDtypeStruct((PL_ROWS, 128), F32),
            jax.ShapeDtypeStruct((PR_ROWS, 128), F32),
            jax.ShapeDtypeStruct((5, OWN, 128), F32),
        ),
        in_specs=[smem] + vmem(10),
        out_specs=tuple(vmem(3)),
        name="pack",
    )(cost_map[0], nodes, slots, pst, hrd, mod, inv, dis, vel, load, mass)
    halo_l = shift(to_right, 1)
    halo_r = shift(to_left, -1)
    dis_out, vel_out, send = pl.pallas_call(
        step_kernel,
        out_shape=(
            jax.ShapeDtypeStruct((5, 8, 128), F32),
            jax.ShapeDtypeStruct((5, 8, 128), F32),
            jax.ShapeDtypeStruct((32, 20, 128), F32),
        ),
        in_specs=[smem] + vmem(11),
        out_specs=tuple(vmem(3)),
        scratch_shapes=[
            pltpu.VMEM((COMP * ROWS, 128), F32),
            pltpu.VMEM((15, 32, 128), F32),
            pltpu.VMEM((NPAD, 128), F32),
            pltpu.VMEM((ROWS, 256, 384), BF16),
            pltpu.VMEM((5, 56, 128), F32),
            pltpu.VMEM((3, 64, 128), F32),
            pltpu.VMEM((2, NPAD, 8, 128), F32),
            pltpu.VMEM((8 * NPAD, 128), F32),
        ],
        compiler_params=pltpu.CompilerParams(vmem_limit_bytes=40 << 20),
        name="steps",
    )(migration_plan[0, :, 0], halo_l, halo_r, own, pst, hrd, mod, inv, dis, vel, load, mass)
    recv = lax.all_to_all(send, "grp", split_axis=0, concat_axis=0, tiled=True)
    res_p, res_h = pl.pallas_call(
        unpack_kernel,
        out_shape=(
            jax.ShapeDtypeStruct((3, 5, 32, 128), F32),
            jax.ShapeDtypeStruct((5, 32, 128), F32),
        ),
        in_specs=vmem(1),
        out_specs=tuple(vmem(2)),
        name="unpack",
    )(recv)
    return (
        dis_out.reshape(1, 5, 1024),
        vel_out.reshape(1, 5, 1024),
        jnp.transpose(res_p, (2, 0, 1, 3))[None],
        jnp.transpose(res_h, (1, 0, 2))[None],
    )


def solution(mesh):
    return jax.shard_map(
        on_device,
        mesh=mesh,
        in_specs=(
            P("span", None, "grp"),
            P("span", None, "grp"),
            P("span", None, "grp"),
            P("span", "grp"),
            P("span", "grp", None, None, None),
            P("span", "grp", None, None),
            P("span", "grp", None, None),
            P("span", "grp", None),
            P("span", None),
            P("span", None, None),
            P("span", None, None),
            P("span", None, None, None),
        ),
        out_specs=(
            P("span", None, "grp"),
            P("span", None, "grp"),
            P("span", "grp", None, None, None),
            P("span", "grp", None, None),
        ),
        check_vma=False,
    )
```

time: 211 us -> 64.5 us (0.31)
  local copies, waits for them, and re-layouts: 79.1 us -> 2.84 us
  starting transfers between devices: 50.7 us -> 9.89 us
  matrix products: 27.4 us -> 0 us
  blocking collectives: 0 us -> 25.7 us
  other arithmetic: 25.3 us -> 0 us
  waiting for transfers between devices: 25.9 us -> 4.06 us
  Pallas kernels: 0 us -> 20.9 us
    gather x2 -> x0, local copies, waits for them, and re-layouts: 65 us -> none  [block_tables(): corner_nodes = jnp.take_along_axis(nodes, slots.reshape(count, -1), axis=1)]
    dot_general x10 -> x0, matrix products: 27.4 us -> none  [the longest x4 15.3 us: element_forces(): nodal = jnp.einsum('cbk,bwk->cbw', forces, tables, precision=HIGHEST)]
    all_to_all x0 -> x1, blocking collectives: none -> 25.7 us  [on_device(): recv = lax.all_to_all(send, 'grp', split_axis=0, concat_axis=0, tiled=True)]
    all_to_all x2 -> x0, starting transfers between devices: 24.2 us -> none  [the longest x1 15.4 us: on_device(): lax.all_to_all(pack(pick, harden), 'grp', split_axis=0, concat_axis=0, ti...]
    ppermute x8 -> x2, waiting for transfers between devices: 25.8 us -> 4.06 us  [shift(): return lax.ppermute(shard, ('span', 'grp'), pairs)]
    pallas_call x0 -> x3, Pallas kernels: none -> 20.9 us  [the longest x1 17 us: on_device(): pl.pallas_call(step_kernel, out_shape=(jax.ShapeDtypeStruct((5, 8, 128),...]
    ppermute x8 -> x2, starting transfers between devices: 26.5 us -> 9.89 us  [shift(): return lax.ppermute(shard, ('span', 'grp'), pairs)]
    another operation x24 -> x0, other arithmetic: 9.54 us -> none
  transfers between devices with their start and end apart: 10 -> 2, of which waited for: 8 -> 1; matrix products, arithmetic and copies ran while one was open for 41% -> 0% of each run, Pallas kernels for 0% -> 0%
where the time goes in v1:
time: 64.5 us; the launch traced here: 64.1 us
  blocking collectives  25.7 us (40%)
  Pallas kernels  20.9 us (32%)
  starting transfers between devices  9.89 us (15%)
  waiting for transfers between devices  4.06 us (6%)
  local copies, waits for them, and re-layouts  2.84 us (4%)
  between operations  0.76 us (1%)
    all_to_all x1, blocking collectives, on_device(): recv = lax.all_to_all(send, 'grp', split_axis=0, concat_axis=0, tiled=True)  25.7 us
    pallas_call x1, Pallas kernels, on_device(): pl.pallas_call(step_kernel, out_shape=(jax.ShapeDtypeStruct((5, 8, 128),...  17 us
    ppermute x2, starting transfers between devices, shift(): return lax.ppermute(shard, ('span', 'grp'), pairs)  9.89 us
    ppermute x2, waiting for transfers between devices, shift(): return lax.ppermute(shard, ('span', 'grp'), pairs)  4.06 us
    pallas_call x1, Pallas kernels, on_device(): pl.pallas_call(pack_kernel, out_shape=(jax.ShapeDtypeStruct((PL_ROWS, 128...  1.98 us
    pallas_call x1, Pallas kernels, on_device(): pl.pallas_call(unpack_kernel, out_shape=(jax.ShapeDtypeStruct((3, 5, 32,...  1.88 us
    dynamic_slice x1, local copies, waits for them, and re-layouts, on_device(): nodes = lax.dynamic_slice_in_dim(block_nodes[0], member * OWN, OWN, 0)  1.41 us
  transfers between devices with their start and end apart: 2, of which 1 were waited for; matrix products, arithmetic and copies ran while one was open for 0% of the time, Pallas kernels for 0%

profile of v1, /device:TPU:193, one launch (start us, length us, event | category | flops | bytes accessed | tf_op | source)
XLA Modules:
  0.0 64.1 jit_solution(4007398310604185606)
XLA Ops:
  0.6 0.0 copy-start
  0.7 1.4 %dynamic-slice_bitcast_fusion.1.nodes = s32[16,256]{1,0:T(8,128)} fusion(s32[1,512,256]{2,1,0:T(8,128)} %param.22, s32[]{:T(128)S(6)} %select_n.4), kind=kLoop, calls=%fused_computation.1 | loop fusion | bytes 32772 | tf_op jit(solution)/shard_map/dynamic_slice | solution.py:316
  2.1 0.0 copy-done
  2.1 0.6 dynamic-slice_bitcast_fusion.slots
  2.7 0.0 copy-start.1
  2.7 0.0 copy-start.2
  2.7 0.0 copy-start.3
  2.7 0.0 copy-start.4
  2.7 0.0 copy-start.5
  2.7 0.0 copy-start.6
  2.7 0.0 copy-start.8
  2.7 2.0 %pack.1 = (f32[472,128]{1,0:T(8,128)}, f32[376,128]{1,0:T(8,128)}, f32[5,16,128]{2,1,0:T(8,128)}) custom-call(s32[512]{0:T(512)} %bitcast.45, s32[16,256]{1,0:T(8,128)} %dynamic-slice_bitcast_fusion.1.nodes, s32[16,4,128]{2,1,0:T(4,128)} %dynamic-slice_bitcast_fusion.slots, f32[3,5,16,128]{3,2,1,0:T(8,128)} %bitcast.28, f32[5,16,128]{2,1,0:T(8,128)} %bitcast.30, ...), custom_call_target="tpu_custom_call" | custom-call | tf_op jit(solution)/shard_map/pack/pallas_call | solution.py:319
  4.7 0.0 copy-start.9
  4.7 3.2 %collective-permute-start = (f32[472,128]{1,0:T(8,128)}, f32[472,128]{1,0:T(8,128)S(1)}, u32[]{:S(2)}, u32[]{:S(2)}) collective-permute-start(f32[472,128]{1,0:T(8,128)} %get-tuple-element.12), channel_id=1, source_target_pairs={{0,1},{1,2},{2,3},{3,4},{4,5},{5,6},{6,7},{7,8},{8,9},{9,10},{10,1... | collective-permute-start | bytes 725000 | tf_op jit(solution)/shard_map/ppermute | solution.py:36
  7.9 0.0 copy-start.10
  8.0 6.7 %collective-permute-start.1 = (f32[376,128]{1,0:T(8,128)}, f32[376,128]{1,0:T(8,128)S(1)}, u32[]{:S(2)}, u32[]{:S(2)}) collective-permute-start(f32[376,128]{1,0:T(8,128)} %get-tuple-element.13), channel_id=1, source_target_pairs={{1,0},{2,1},{3,2},{4,3},{5,4},{6,5},{7,6},{8,7},{9,8},{10,9},{11,1... | collective-permute-start | bytes 577544 | tf_op jit(solution)/shard_map/ppermute | solution.py:36
  14.6 4.1 %collective-permute-done.1.halo_r = f32[376,128]{1,0:T(8,128)S(1)} collective-permute-done((f32[376,128]{1,0:T(8,128)}, f32[376,128]{1,0:T(8,128)S(1)}, u32[]{:S(2)}, u32[]{:S(2)}) %collective-permute-start.1) | collective-permute-done | bytes 192544 | tf_op jit(solution)/shard_map/ppermute | solution.py:36
  18.7 0.0 collective-permute-done.halo_l
  18.7 0.0 copy-done.1
  18.7 0.0 copy-done.2
  18.7 0.0 copy-done.3
  18.7 0.0 copy-done.4
  18.7 0.0 copy-done.5
  18.7 0.0 copy-done.6
  18.7 0.0 copy-done.8
  18.7 0.0 copy-done.9
  18.7 0.0 copy-done.10
  18.8 0.0 copy-start.7
  18.8 0.8 %copy-done.7 = f32[5,16,128]{2,1,0:T(8,128)S(1)} copy-done((f32[5,16,128]{2,1,0:T(8,128)S(1)}, f32[5,16,128]{2,1,0:T(8,128)}, u32[]{:S(2)}) %copy-start.7) | copy-done | bytes 40984
  19.5 17.0 %steps.1 = (f32[5,8,128]{2,1,0:T(8,128)}, f32[5,8,128]{2,1,0:T(8,128)}, f32[32,20,128]{2,1,0:T(8,128)S(1)}) custom-call(s32[512]{0:T(512)S(1)} %bitcast.44, f32[472,128]{1,0:T(8,128)S(1)} %collective-permute-done.halo_l, f32[376,128]{1,0:T(8,128)S(1)} %collective-permute-done.1.halo_r, f32[5,16,128]{2,1,0:T(8,128)S(1)} %copy-done.7, ...), custom_call_target="tpu_custom_call" | custom-call | tf_op jit(solution)/shard_map/steps/pallas_call | solution.py:332
  36.6 25.7 %all_to_all.5.recv = f32[32,20,128]{2,1,0:T(8,128)} all-to-all(f32[32,20,128]{2,1,0:T(8,128)S(1)} %get-tuple-element.17), channel_id=1, replica_groups=mesh['span'=16,'grp'=32] {'grp'}, dimensions={0} | all-to-all | bytes 655360 | tf_op jit(solution)/shard_map/all_to_all | solution.py:354
  62.2 1.9 %unpack.1 = (f32[3,5,32,128]{3,2,1,0:T(8,128)}, f32[5,32,128]{2,1,0:T(8,128)}) custom-call(f32[32,20,128]{2,1,0:T(8,128)} %all_to_all.5.recv), custom_call_target="tpu_custom_call" | custom-call | tf_op jit(solution)/shard_map/unpack/pallas_call | solution.py:355
Async XLA Ops:
  0.6 1.4 %copy-start = (s32[1,512,4,128]{3,2,1,0:T(4,128)S(1)}, s32[1,512,4,128]{3,2,1,0:T(4,128)}, u32[]{:S(2)}) copy-start(s32[1,512,4,128]{3,2,1,0:T(4,128)} %param.23) | copy-start | bytes 3145732
  2.7 16.0 %copy-start.1 = (f32[1,16,3,5,128]{4,1,3,2,0:T(8,128)S(1)}, f32[1,16,3,5,128]{4,1,3,2,0:T(8,128)}, u32[]{:S(2)}) copy-start(f32[1,16,3,5,128]{4,1,3,2,0:T(8,128)} %param.16) | copy-start | bytes 368644
  2.7 16.0 %copy-start.2 = (f32[1,16,5,128]{3,1,2,0:T(8,128)S(1)}, f32[1,16,5,128]{3,1,2,0:T(8,128)}, u32[]{:S(2)}) copy-start(f32[1,16,5,128]{3,1,2,0:T(8,128)} %param.17) | copy-start | bytes 122884
  2.7 16.0 %copy-start.3 = (f32[1,16,5,128]{3,1,2,0:T(8,128)S(1)}, f32[1,16,5,128]{3,1,2,0:T(8,128)}, u32[]{:S(2)}) copy-start(f32[1,16,5,128]{3,1,2,0:T(8,128)} %param.18) | copy-start | bytes 122884
  2.7 16.0 %copy-start.4 = (f32[1,5,1024]{2,0,1:T(1,128)S(1)}, f32[1,5,1024]{2,0,1:T(1,128)}, u32[]{:S(2)}) copy-start(f32[1,5,1024]{2,0,1:T(1,128)} %param.12) | copy-start | bytes 61444
  2.7 16.0 %copy-start.5 = (f32[1,5,1024]{2,0,1:T(1,128)S(1)}, f32[1,5,1024]{2,0,1:T(1,128)}, u32[]{:S(2)}) copy-start(f32[1,5,1024]{2,0,1:T(1,128)} %param.13) | copy-start | bytes 61444
  2.7 16.0 %copy-start.6 = (f32[1,5,1024]{2,0,1:T(1,128)S(1)}, f32[1,5,1024]{2,0,1:T(1,128)}, u32[]{:S(2)}) copy-start(f32[1,5,1024]{2,0,1:T(1,128)} %param.14) | copy-start | bytes 61444
  2.7 16.0 %copy-start.8 = (f32[1,16,128]{2,1,0:T(8,128)S(1)}, f32[1,16,128]{2,1,0:T(8,128)}, u32[]{:S(2)}) copy-start(f32[1,16,128]{2,1,0:T(8,128)} %param.19) | copy-start | bytes 24580
  4.7 14.0 %copy-start.9 = (f32[1,1024]{1,0:T(1,128)S(1)}, f32[1,1024]{1,0:T(1,128)}, u32[]{:S(2)}) copy-start(f32[1,1024]{1,0:T(1,128)} %param.15) | copy-start | bytes 12292
  4.7 14.0 %collective-permute-start = (f32[472,128]{1,0:T(8,128)}, f32[472,128]{1,0:T(8,128)S(1)}, u32[]{:S(2)}, u32[]{:S(2)}) collective-permute-start(f32[472,128]{1,0:T(8,128)} %get-tuple-element.12), channel_id=1, source_target_pairs={{0,1},{1,2},{2,3},{3,4},{4,5},{5,6},{6,7},{7,8},{8,9},{9,10},{10,1... | collective-permute-start | bytes 725000 | tf_op jit(solution)/shard_map/ppermute | solution.py:36
  7.9 10.8 %copy-start.10 = (s32[1,512,1]{1,2,0:T(1,128)S(1)}, s32[1,512,1]{1,2,0:T(1,128)}, u32[]{:S(2)}) copy-start(s32[1,512,1]{1,2,0:T(1,128)} %param.21) | copy-start | bytes 6148
  8.0 10.7 %collective-permute-start.1 = (f32[376,128]{1,0:T(8,128)}, f32[376,128]{1,0:T(8,128)S(1)}, u32[]{:S(2)}, u32[]{:S(2)}) collective-permute-start(f32[376,128]{1,0:T(8,128)} %get-tuple-element.13), channel_id=1, source_target_pairs={{1,0},{2,1},{3,2},{4,3},{5,4},{6,5},{7,6},{8,7},{9,8},{10,9},{11,1... | collective-permute-start | bytes 577544 | tf_op jit(solution)/shard_map/ppermute | solution.py:36
  18.8 0.8 %copy-start.7 = (f32[5,16,128]{2,1,0:T(8,128)S(1)}, f32[5,16,128]{2,1,0:T(8,128)}, u32[]{:S(2)}) copy-start(f32[5,16,128]{2,1,0:T(8,128)} %get-tuple-element.14.own) | copy-start | bytes 122884

commit v2 on v1

v2 whole, which is shorter than its diff:
```python
import math

import jax
import jax.numpy as jnp
from jax import lax
from jax.experimental import pallas as pl
from jax.experimental.pallas import tpu as pltpu
from jax.sharding import PartitionSpec as P

NEWTON = 4
STEPS = 4
POISSON = 0.3
YIELD = 0.1
SATURATE = 0.1
RATE = 20.0
STEP_TIME = 0.25
THROUGH = (1.0 / 12, 4.0 / 12, 2.0 / 12, 4.0 / 12, 1.0 / 12)

OWN = 16
LEFT = 12
RIGHT = 9
BLOCKS = LEFT + OWN + RIGHT
ROWS = 40
NROW = 20
NPAD = 24
COMP = 31
PL_ROWS = 472
PR_ROWS = 376
C_H, C_M, C_Z, C_I, C_C = 15, 20, 25, 26, 30
F32 = jnp.float32
BF16 = jnp.bfloat16


def shift(shard, by):
    size = lax.axis_size(("span", "grp"))
    pairs = [(i, i + by) for i in range(size) if 0 <= i + by < size]
    return lax.ppermute(shard, ("span", "grp"), pairs)


def lanes(values, index):
    return jnp.take_along_axis(values, index, axis=1)


def pack_kernel(
    cost, nodes_all, slots_all, pst, hrd, mod, inv, dis, vel, load, mass,
    to_right, to_left, own,
    nodes, slots, sems,
):
    first = pl.multiple_of(lax.axis_index("grp") * OWN, OWN)
    fetch_nodes = pltpu.make_async_copy(nodes_all.at[pl.ds(first, OWN)], nodes, sems.at[0])
    fetch_slots = pltpu.make_async_copy(slots_all.at[pl.ds(first, OWN)], slots, sems.at[1])
    fetch_nodes.start()
    fetch_slots.start()
    for j in range(OWN):
        own[4, j : j + 1, :] = jnp.full((1, 128), cost[first + j], jnp.int32).astype(F32)
    def rows_of(c, at, count):
        if c < 15:
            return pst[c // 5, c % 5, at : at + count, :]
        if c < 20:
            return hrd[c - 15, at : at + count, :]
        if c < 25:
            return mod[c - 20, at : at + count, :]
        if c == 25:
            return inv[at : at + count, :]
        return own[c - 26, at : at + count, :]

    for c in range(C_I):
        to_right[c * LEFT : (c + 1) * LEFT, :] = rows_of(c, OWN - LEFT, LEFT)
        to_left[c * RIGHT : (c + 1) * RIGHT, :] = rows_of(c, 0, RIGHT)
    for i in range(16):
        source = (dis, vel, load)[i // 5] if i < 15 else mass
        values = source[i % 5] if i < 15 else source[...]
        to_right[COMP * LEFT + 6 * i : COMP * LEFT + 6 * i + 6, :] = values[2:8]
        to_left[COMP * RIGHT + 6 * i : COMP * RIGHT + 6 * i + 6, :] = values[0:6]
    fetch_nodes.wait()
    fetch_slots.wait()
    for o in range(2):
        rows = slice(8 * o, 8 * o + 8)
        low, high = nodes[rows, 0:128], nodes[rows, 128:256]
        base = (first + 8 * o + lax.broadcasted_iota(jnp.int32, (8, 128), 0)) * 64
        for k in range(4):
            slot = slots[rows, k, :]
            lane = slot & 127
            node = jnp.where(slot < 128, lanes(low, lane), lanes(high, lane))
            own[k, rows, :] = (node - base).astype(F32)

    for c in range(C_I, COMP):
        to_right[c * LEFT : (c + 1) * LEFT, :] = rows_of(c, OWN - LEFT, LEFT)
        to_left[c * RIGHT : (c + 1) * RIGHT, :] = rows_of(c, 0, RIGHT)


SLOPE = -RATE * math.log2(math.e)
DIAG = 1.0 - POISSON + POISSON * POISSON
CROSS = (4.0 * POISSON - 1.0 - POISSON * POISSON) / DIAG
SHEAR = 3.0 * (0.5 * (1.0 - POISSON)) ** 2 / DIAG
ELASTIC = 1.0 / (1.0 - POISSON * POISSON)
TRIPLE = 1.5 / (1.0 + POISSON)


def element_octet(disp, state, costs, inv):
    half = 0.5 * inv
    lean = [u[1] - u[3] for u in disp]
    rise = [u[2] - u[0] for u in disp]
    dx = [half * (s + t) for s, t in zip(lean, rise)]
    dy = [half * (t - s) for s, t in zip(lean, rise)]
    mean_a = 0.25 * ((disp[3][0] + disp[3][1]) + (disp[3][2] + disp[3][3]))
    mean_b = 0.25 * ((disp[4][0] + disp[4][1]) + (disp[4][2] + disp[4][3]))
    membrane = (dx[0], dy[1], dy[0] + dx[1])
    bending = (dx[3], dy[4], dy[3] + dx[4])
    shear = (dx[2] + mean_a, dy[2] + mean_b)
    far = [0.5 * b for b in bending]
    near = [0.25 * b for b in bending]
    fibre = (
        [m - b for m, b in zip(membrane, far)],
        [m - b for m, b in zip(membrane, near)],
        membrane,
        [m + b for m, b in zip(membrane, near)],
        [m + b for m, b in zip(membrane, far)],
    )
    active = [costs > float(t) for t in range(NEWTON)]
    offset = 0.5 * SATURATE * SLOPE
    new_state = []
    load = []
    g3_sum = None
    for p in range(5):
        plastic, level, g3 = state[p]
        e0, e1, e2 = [fibre[p][i] - plastic[i] for i in range(3)]
        square = e1 * (e1 + CROSS * e0) + e0 * e0 + SHEAR * (e2 * e2)
        norm = square * lax.rsqrt(jnp.maximum(square, 1e-37))
        q = (g3 * norm) * (SLOPE * ELASTIC / TRIPLE * math.sqrt(DIAG))
        base = q - SLOPE * (YIELD + SATURATE)
        decay = jnp.exp2(level)
        top = base + offset * decay
        flows = top < 0.0
        step = top / (g3 + decay)
        for turn in range(1, NEWTON):
            decay = jnp.exp2(level + step)
            moved = (base + decay * (step + offset)) / (g3 + decay)
            step = jnp.where(active[turn], moved, step)
        step = jnp.where(flows, step, 0.0)
        loss = (g3 * step) / jnp.minimum(q, SLOPE * YIELD)
        new_state.append(([plastic[0] + loss * e0, plastic[1] + loss * e1, plastic[2] + loss * e2], level + step))
        scale = (g3 * (THROUGH[p] * ELASTIC / TRIPLE)) * (1.0 - loss)
        load.append([scale * e0, scale * e1, scale * e2])
        part = THROUGH[p] * g3
        g3_sum = part if g3_sum is None else g3_sum + part
    force = [((load[0][i] + load[4][i]) + (load[1][i] + load[3][i])) + load[2][i] for i in range(3)]
    moment = [0.5 * (load[4][i] - load[0][i]) + 0.25 * (load[3][i] - load[1][i]) for i in range(3)]

    def resultant(s):
        a, b, c = half * s[0], half * s[1], half * s[2]
        return a + POISSON * b, POISSON * a + b, (0.5 * (1.0 - POISSON)) * c

    shear_modulus = g3_sum * (5.0 / 6.0 / (2.0 * (1.0 + POISSON)) / TRIPLE)
    q0, q1 = shear_modulus * shear[0], shear_modulus * shear[1]
    n0, n1, n2 = resultant(force)
    m0, m1, m2 = resultant(moment)
    k0, k1 = half * q0, half * q1
    lean_part = (n0 - n2, n2 - n1, k0 - k1, m0 - m2, m2 - m1)
    rise_part = (n0 + n2, n2 + n1, k0 + k1, m0 + m2, m2 + m1)
    even = (None, None, None, 0.25 * q0, 0.25 * q1)
    return new_state, (lean_part, rise_part, even)


def build_tables(corner_row, count, tab, spot, off):
    spot[...] = lax.broadcasted_iota(jnp.int32, (256, 256), 0).astype(F32).astype(BF16)

    def spread(b, _):
        for k, place in ((1, 0), (2, 1), (3, 2), (0, 3)):
            row = jnp.broadcast_to(corner_row(k, b), (8, 128))
            off[b, :, 128 * place : 128 * place + 128] = row.astype(BF16)
        return 0

    lax.fori_loop(0, count, spread, 0, unroll=min(4, count) if count % 4 == 0 else 3)

    def build(b, _):
        one, zero = jnp.ones((8, 256), BF16), jnp.zeros((8, 256), BF16)
        first, second = off[b, :, 0:256], off[b, :, 256:512]
        for r in range(32):
            rows = slice(8 * r, 8 * r + 8)
            here = spot[rows, :]
            hit = jnp.where(here == first, one, zero)
            miss = jnp.where(here == second, one, zero)
            tab[b, rows, 0:256] = hit - miss
            both = hit + miss
            tab[b, rows, 256:384] = both[:, 0:128] + both[:, 128:256]
        return 0

    lax.fori_loop(0, count, build, 0)


def table_kernel(own, tab, spot, off):
    build_tables(lambda k, b: own[k, pl.ds(b, 1), :], OWN, tab, spot, off)


def step_kernel(
    plan, halo_l, halo_r, own, tab_own, pst, hrd, mod, inv, dis, vel, load, mass,
    dis_out, vel_out, send,
    st, nd, rm, tab, win, grp, itn, spot, off,
):
    for c in range(COMP):
        if c < 15:
            mine = pst[c // 5, c % 5]
        elif c < 20:
            mine = hrd[c - 15]
        elif c < 25:
            mine = mod[c - 20]
        elif c == 25:
            mine = inv[...]
        else:
            mine = own[c - 26]
        at = c * ROWS
        scale, bias = 1.0, 0.0
        if C_H <= c < C_M:
            scale, bias = SLOPE, 1.0
        elif C_M <= c < C_Z:
            scale = TRIPLE
        st[at : at + LEFT, :] = halo_l[c * LEFT : (c + 1) * LEFT, :] * scale + bias
        st[at + LEFT : at + LEFT + OWN, :] = mine * scale + bias
        st[at + LEFT + OWN : at + BLOCKS, :] = halo_r[c * RIGHT : (c + 1) * RIGHT, :] * scale + bias
        st[at + BLOCKS : at + ROWS, :] = jnp.zeros((ROWS - BLOCKS, 128), F32)
    pinned = (lax.axis_index("span") == 0) & (lax.axis_index("grp") == 0)
    free_rows = jnp.where(
        pinned & (lax.broadcasted_iota(jnp.int32, (8, 128), 0) < 2), 0.0, 1.0
    ).astype(F32)
    for i in range(16):
        left = halo_l[COMP * LEFT + 6 * i : COMP * LEFT + 6 * i + 6, :]
        right = halo_r[COMP * RIGHT + 6 * i : COMP * RIGHT + 6 * i + 6, :]
        if i < 15:
            mine = (dis, vel, load)[i // 5][i % 5]
            if 5 <= i < 10:
                mine = mine * free_rows
            nd[i, 0:6, :] = left
            nd[i, 6:14, :] = mine
            nd[i, 14:20, :] = right
            nd[i, 20:32, :] = jnp.zeros((12, 128), F32)
        else:
            rm[0:6, :] = left
            rm[6:14, :] = mass[...]
            rm[14:20, :] = right
            rm[20:24, :] = jnp.zeros((4, 128), F32)
    weight = rm[...]
    there = weight > 0.0
    weight = jnp.where(there, STEP_TIME / jnp.where(there, weight, 1.0), 0.0)
    rm[...] = weight
    rm[6:14, :] = rm[6:14, :] * free_rows
    grp[...] = jnp.zeros(grp.shape, F32)

    def halo_row(k, b):
        return st[pl.ds((C_I + k) * ROWS + jnp.where(b < LEFT, b, b + OWN), 1), :]

    build_tables(halo_row, LEFT + RIGHT, tab, spot, off)

    def table(b):
        if b < LEFT:
            return tab[b]
        return tab_own[b - LEFT] if b < LEFT + OWN else tab[b - OWN]

    lane = lax.broadcasted_iota(jnp.int32, (NPAD, 128), 1)

    half_lane = lax.broadcasted_iota(jnp.int32, (8, 128), 1) < 64

    def comp(c, o):
        return st[c * ROWS + 8 * o : c * ROWS + 8 * o + 8, :]

    def update(o):
        at = 8 * o
        index = [comp(C_I + k, o).astype(jnp.int32) for k in range(4)]
        near = [i < 128 for i in index]
        place = [i & 127 for i in index]
        disp = []
        for d in range(5):
            low = win[d, at : at + 8, :]
            high = win[d, at + 2 : at + 10, :]
            disp.append([jnp.where(near[k], lanes(low, place[k]), lanes(high, place[k])) for k in range(4)])
        state = [([comp(i * 5 + p, o) for i in range(3)], comp(C_H + p, o), comp(C_M + p, o)) for p in range(5)]
        new_state, parts = element_octet(disp, state, comp(C_C, o), comp(C_Z, o))
        for p in range(5):
            plastic, level = new_state[p]
            for i in range(3):
                st[(i * 5 + p) * ROWS + at : (i * 5 + p) * ROWS + at + 8, :] = plastic[i]
            st[(C_H + p) * ROWS + at : (C_H + p) * ROWS + at + 8, :] = level
        for s in range(3):
            for d in range(5):
                if parts[s][d] is not None:
                    grp[o, s, pl.ds(d, 8, stride=8), :] = parts[s][d]

    def assemble(o, totals, first, last):
        for j in range(8):
            b = 8 * o + j
            if not first <= b < last:
                continue
            values = jnp.concatenate([grp[o, s, 8 * j : 8 * j + 8, :] for s in range(3)], axis=1)
            high = values.astype(BF16)
            low = (values - high.astype(F32)).astype(BF16)
            both = jnp.concatenate([high, low], axis=0)
            out = lax.dot_general(both, table(b), (((1,), (1,)), ((), ())), preferred_element_type=F32)
            out = out[0:8] + out[8:16]
            for h in range(2):
                piece = out[:, 128 * h : 128 * h + 128]
                place = (j % 2, b // 2 + h)
                totals[place] = piece if place not in totals else totals[place] + piece

    itn[...] = jnp.zeros(itn.shape, F32)
    for t in range(STEPS):
        reach_l, reach_r = 3 * (STEPS - t), 3 * (STEPS - t - 1)
        first, last = LEFT - reach_l, LEFT + OWN + reach_r
        for d in range(5):
            here = nd[d, 0:NPAD, :]
            rolled = pltpu.roll(here, 64, 1)
            after = pltpu.roll(nd[d, 1 : NPAD + 1, :], 64, 1)
            win[d, pl.ds(0, NPAD, stride=2), :] = here
            win[d, pl.ds(1, NPAD, stride=2), :] = jnp.where(lane < 64, rolled, after)
        totals = {}
        for o in range(first // 8, (last + 7) // 8):
            update(o)
            assemble(o, totals, first, last)
        zero = jnp.zeros((8, 128), F32)
        before = zero
        for r in range(NROW):
            odd = pltpu.roll(totals[1, r], 64, 1) if (1, r) in totals else zero
            itn[pl.ds(r, 8, stride=NPAD), :] = totals.get((0, r), zero) + jnp.where(half_lane, before, odd)
            before = odd
        weight = rm[...]
        for d in range(5):
            speed = nd[5 + d, 0:NPAD, :] + weight * (nd[10 + d, 0:NPAD, :] - itn[d * NPAD : (d + 1) * NPAD, :])
            nd[5 + d, 0:NPAD, :] = speed
            nd[d, 0:NPAD, :] = nd[d, 0:NPAD, :] + STEP_TIME * speed

    for d in range(5):
        dis_out[d] = nd[d, 6:14, :]
        vel_out[d] = nd[5 + d, 6:14, :]
    send[...] = jnp.zeros(send.shape, F32)
    for p in range(5):
        rows = slice((C_H + p) * ROWS + LEFT, (C_H + p) * ROWS + LEFT + OWN)
        st[rows, :] = (st[rows, :] - 1.0) * (1.0 / SLOPE)
    first = lax.axis_index("grp") * OWN
    for j in range(OWN):
        for q in range(5):
            send[plan[first + j], q] = st[pl.ds(4 * q * ROWS + LEFT + j, 4, stride=ROWS), :]


def unpack_kernel(recv, pst, hrd):
    for g in range(32):
        for q in range(5):
            values = recv[g, q]
            if q < 3:
                pst[pl.ds(128 * q + g, 4, stride=32), :] = values
            elif q == 3:
                pst[pl.ds(384 + g, 3, stride=32), :] = values[0:3]
                hrd[pl.ds(g, 1), :] = values[3:4]
            else:
                hrd[pl.ds(32 + g, 4, stride=32), :] = values


def vmem(count):
    return [pl.BlockSpec(memory_space=pltpu.VMEM) for _ in range(count)]


def on_device(
    displacement,
    velocity,
    nodal_load,
    nodal_mass,
    plastic_strain,
    hardening,
    ply_modulus,
    inverse_size,
    cost_map,
    migration_plan,
    block_nodes,
    corner_slot,
):
    dis = displacement.reshape(5, 8, 128)
    vel = velocity.reshape(5, 8, 128)
    load = nodal_load.reshape(5, 8, 128)
    mass = nodal_mass.reshape(8, 128)
    pst = jnp.transpose(plastic_strain[0], (1, 2, 0, 3))
    hrd = jnp.transpose(hardening[0], (1, 0, 2))
    mod = jnp.transpose(ply_modulus[0], (1, 0, 2))
    inv = inverse_size[0]
    smem = pl.BlockSpec(memory_space=pltpu.SMEM)
    hbm = pl.BlockSpec(memory_space=pltpu.HBM)
    to_right, to_left, own = pl.pallas_call(
        pack_kernel,
        out_shape=(
            jax.ShapeDtypeStruct((PL_ROWS, 128), F32),
            jax.ShapeDtypeStruct((PR_ROWS, 128), F32),
            jax.ShapeDtypeStruct((5, OWN, 128), F32),
        ),
        in_specs=[smem, hbm, hbm] + vmem(8),
        out_specs=tuple(vmem(3)),
        scratch_shapes=[
            pltpu.VMEM((OWN, 256), jnp.int32),
            pltpu.VMEM((OWN, 4, 128), jnp.int32),
            pltpu.SemaphoreType.DMA((2,)),
        ],
        compiler_params=pltpu.CompilerParams(vmem_limit_bytes=60 * 1024 * 1024),
        name="pack",
    )(cost_map[0], block_nodes[0], corner_slot[0], pst, hrd, mod, inv, dis, vel, load, mass)
    tab_own = pl.pallas_call(
        table_kernel,
        out_shape=jax.ShapeDtypeStruct((OWN, 256, 384), BF16),
        in_specs=vmem(1),
        out_specs=vmem(1)[0],
        scratch_shapes=[pltpu.VMEM((256, 256), BF16), pltpu.VMEM((OWN, 8, 512), BF16)],
        compiler_params=pltpu.CompilerParams(vmem_limit_bytes=8 << 20),
        cost_estimate=pl.CostEstimate(flops=20_000_000, bytes_accessed=6_000_000, transcendentals=0),
        name="tables",
    )(own)
    halo_l = shift(to_right, 1)
    halo_r = shift(to_left, -1)
    dis_out, vel_out, send = pl.pallas_call(
        step_kernel,
        out_shape=(
            jax.ShapeDtypeStruct((5, 8, 128), F32),
            jax.ShapeDtypeStruct((5, 8, 128), F32),
            jax.ShapeDtypeStruct((32, 5, 4, 128), F32),
        ),
        in_specs=[smem] + vmem(12),
        out_specs=tuple(vmem(3)),
        scratch_shapes=[
            pltpu.VMEM((COMP * ROWS, 128), F32),
            pltpu.VMEM((15, 32, 128), F32),
            pltpu.VMEM((NPAD, 128), F32),
            pltpu.VMEM((LEFT + RIGHT, 256, 384), BF16),
            pltpu.VMEM((5, 56, 128), F32),
            pltpu.VMEM((ROWS // 8, 3, 64, 128), F32),
            pltpu.VMEM((8 * NPAD, 128), F32),
            pltpu.VMEM((256, 256), BF16),
            pltpu.VMEM((LEFT + RIGHT, 8, 512), BF16),
        ],
        compiler_params=pltpu.CompilerParams(vmem_limit_bytes=24 << 20),
        name="steps",
    )(migration_plan[0, :, 0], halo_l, halo_r, own, tab_own, pst, hrd, mod, inv, dis, vel, load, mass)
    recv = lax.all_to_all(send, "grp", split_axis=0, concat_axis=0, tiled=True)
    res_p, res_h = pl.pallas_call(
        unpack_kernel,
        out_shape=(
            jax.ShapeDtypeStruct((480, 128), F32),
            jax.ShapeDtypeStruct((160, 128), F32),
        ),
        in_specs=vmem(1),
        out_specs=tuple(vmem(2)),
        compiler_params=pltpu.CompilerParams(vmem_limit_bytes=4 << 20),
        name="unpack",
    )(recv)
    return (
        dis_out.reshape(1, 5, 1024),
        vel_out.reshape(1, 5, 1024),
        jnp.transpose(res_p.reshape(3, 5, 32, 128), (2, 0, 1, 3))[None],
        jnp.transpose(res_h.reshape(5, 32, 128), (1, 0, 2))[None],
    )


def solution(mesh):
    return jax.shard_map(
        on_device,
        mesh=mesh,
        in_specs=(
            P("span", None, "grp"),
            P("span", None, "grp"),
            P("span", None, "grp"),
            P("span", "grp"),
            P("span", "grp", None, None, None),
            P("span", "grp", None, None),
            P("span", "grp", None, None),
            P("span", "grp", None),
            P("span", None),
            P("span", None, None),
            P("span", None, None),
            P("span", None, None, None),
        ),
        out_specs=(
            P("span", None, "grp"),
            P("span", None, "grp"),
            P("span", "grp", None, None, None),
            P("span", "grp", None, None),
        ),
        check_vma=False,
    )
```

time: 64.5 us -> 53.3 us (0.83)
  Pallas kernels: 20.9 us -> 14.4 us
  local copies, waits for them, and re-layouts: 2.84 us -> 0.81 us
  blocking collectives: 25.7 us -> 24.1 us
  waiting for transfers between devices: 4.06 us -> 2.6 us
    pallas_call x1, Pallas kernels: 17 us -> 9.98 us  [on_device(): pl.pallas_call(step_kernel, out_shape=(jax.ShapeDtypeStruct((5, 8, 128),...]
    dynamic_slice x2 -> x0, local copies, waits for them, and re-layouts: 2.02 us -> none  [the longest x1 1.41 us: on_device(): nodes = lax.dynamic_slice_in_dim(block_nodes[0], member * OWN, OWN, 0)]
    all_to_all x1, blocking collectives: 25.7 us -> 24.1 us  [on_device(): recv = lax.all_to_all(send, 'grp', split_axis=0, concat_axis=0, tiled=True)]
    ppermute x2, waiting for transfers between devices: 4.06 us -> 2.6 us  [shift(): return lax.ppermute(shard, ('span', 'grp'), pairs)]
    pallas_call x1, Pallas kernels: 1.98 us -> 2.76 us  [on_device(): pl.pallas_call(pack_kernel, out_shape=(jax.ShapeDtypeStruct((PL_ROWS, 128...]
    pallas_call x1 -> x2, Pallas kernels: 1.88 us -> 1.68 us  [the longest x1 1 us: on_device(): pl.pallas_call(unpack_kernel, out_shape=(jax.ShapeDtypeStruct((480, 128),...]
  transfers between devices with their start and end apart: 2 -> 2, of which waited for: 1 -> 1; matrix products, arithmetic and copies ran while one was open for 0% -> 0% of each run, Pallas kernels for 0% -> 1%
where the time goes in v2:
time: 53.3 us; the launch traced here: 52.5 us
  blocking collectives  24.1 us (45%)
  Pallas kernels  14.4 us (27%)
  starting transfers between devices  9.77 us (18%)
  waiting for transfers between devices  2.6 us (5%)
  local copies, waits for them, and re-layouts  0.81 us (2%)
  between operations  0.8 us (2%)
    all_to_all x1, blocking collectives, on_device(): recv = lax.all_to_all(send, 'grp', split_axis=0, concat_axis=0, tiled=True)  24.1 us
    pallas_call x1, Pallas kernels, on_device(): pl.pallas_call(step_kernel, out_shape=(jax.ShapeDtypeStruct((5, 8, 128),...  9.98 us
    ppermute x2, starting transfers between devices, shift(): return lax.ppermute(shard, ('span', 'grp'), pairs)  9.77 us
    pallas_call x1, Pallas kernels, on_device(): pl.pallas_call(pack_kernel, out_shape=(jax.ShapeDtypeStruct((PL_ROWS, 128...  2.76 us
    ppermute x2, waiting for transfers between devices, shift(): return lax.ppermute(shard, ('span', 'grp'), pairs)  2.6 us
  transfers between devices with their start and end apart: 2, of which 1 were waited for; matrix products, arithmetic and copies ran while one was open for 0% of the time, Pallas kernels for 1%

profile of v2, /device:TPU:193, one launch (start us, length us, event | category | flops | bytes accessed | tf_op | source)
XLA Modules:
  0.0 52.5 jit_solution(2661610973969473094)
XLA Ops:
  0.6 0.0 copy-start.7
  0.6 0.0 copy-start.2
  0.7 0.0 copy-start.1
  0.7 0.0 copy-start
  0.7 0.0 copy-start.8
  0.7 0.0 copy-start.6
  0.7 0.0 copy-start.5
  0.7 0.0 copy-start.4
  0.7 0.0 copy-start.9
  0.7 2.8 %pack.1 = (f32[472,128]{1,0:T(8,128)}, f32[376,128]{1,0:T(8,128)}, f32[5,16,128]{2,1,0:T(8,128)}) custom-call(s32[512]{0:T(512)} %bitcast.49, s32[512,256]{1,0:T(8,128)} %bitcast.48, s32[512,4,128]{2,1,0:T(4,128)} %bitcast.47, f32[3,5,16,128]{3,2,1,0:T(8,128)} %bitcast.30, f32[5,16,128]{2,1,0:T(8,128)} %bitcast.32, f32[5,16,128]{2,1,0:T(8,128)} %bitcast.34, ...), custom_call_target="tpu_custom_call" | custom-call | tf_op jit(solution)/shard_map/pack/pallas_call | solution.py:384
  3.5 3.1 %collective-permute-start = (f32[472,128]{1,0:T(8,128)}, f32[472,128]{1,0:T(8,128)S(1)}, u32[]{:S(2)}, u32[]{:S(2)}) collective-permute-start(f32[472,128]{1,0:T(8,128)} %get-tuple-element.12), channel_id=1, source_target_pairs={{0,1},{1,2},{2,3},{3,4},{4,5},{5,6},{6,7},{7,8},{8,9},{9,10},{10,1... | collective-permute-start | bytes 725000 | tf_op jit(solution)/shard_map/ppermute | solution.py:37
  6.6 6.7 %collective-permute-start.1 = (f32[376,128]{1,0:T(8,128)}, f32[376,128]{1,0:T(8,128)S(1)}, u32[]{:S(2)}, u32[]{:S(2)}) collective-permute-start(f32[376,128]{1,0:T(8,128)} %get-tuple-element.13), channel_id=1, source_target_pairs={{1,0},{2,1},{3,2},{4,3},{5,4},{6,5},{7,6},{8,7},{9,8},{10,9},{11,1... | collective-permute-start | bytes 577544 | tf_op jit(solution)/shard_map/ppermute | solution.py:37
  13.3 0.0 copy-start.3
  13.3 0.8 %copy-done.3 = f32[5,16,128]{2,1,0:T(8,128)S(1)} copy-done((f32[5,16,128]{2,1,0:T(8,128)S(1)}, f32[5,16,128]{2,1,0:T(8,128)}, u32[]{:S(2)}) %copy-start.3) | copy-done | bytes 40984
  14.1 0.7 %tables.1.tab_own = bf16[16,256,384]{2,1,0:T(8,128)(2,1)S(1)} custom-call(f32[5,16,128]{2,1,0:T(8,128)S(1)} %copy-done.3), custom_call_target="tpu_custom_call" | custom-call | flops 20000000 | bytes 6000000 | tf_op jit(solution)/shard_map/tables/pallas_call | solution.py:401
  14.7 2.6 %collective-permute-done.1.halo_r = f32[376,128]{1,0:T(8,128)S(1)} collective-permute-done((f32[376,128]{1,0:T(8,128)}, f32[376,128]{1,0:T(8,128)S(1)}, u32[]{:S(2)}, u32[]{:S(2)}) %collective-permute-start.1) | collective-permute-done | bytes 192544 | tf_op jit(solution)/shard_map/ppermute | solution.py:37
  17.3 0.0 collective-permute-done.halo_l
  17.3 0.0 copy-done.7
  17.4 0.0 copy-done.2
  17.4 0.0 copy-done.1
  17.4 0.0 copy-done
  17.4 0.0 copy-done.8
  17.4 0.0 copy-done.6
  17.4 0.0 copy-done.5
  17.4 0.0 copy-done.4
  17.4 0.0 copy-done.9
  17.4 10.0 %steps.1 = (f32[5,8,128]{2,1,0:T(8,128)}, f32[5,8,128]{2,1,0:T(8,128)}, f32[32,5,4,128]{3,2,1,0:T(4,128)S(1)}) custom-call(s32[512]{0:T(512)S(1)} %bitcast.46, f32[472,128]{1,0:T(8,128)S(1)} %collective-permute-done.halo_l, f32[376,128]{1,0:T(8,128)S(1)} %collective-permute-done.1.halo_r, f32[5,16,128]{2,1,0:T(8,128)S(1)} %copy-done.3, ...), custom_call_target="tpu_custom_call" | custom-call | tf_op jit(solution)/shard_map/steps/pallas_call | solution.py:413
  27.4 24.1 %all_to_all.5.recv = f32[32,5,4,128]{3,2,1,0:T(4,128)S(1)} all-to-all(f32[32,5,4,128]{3,2,1,0:T(4,128)S(1)} %get-tuple-element.17), channel_id=1, replica_groups=mesh['span'=16,'grp'=32] {'grp'}, dimensions={0} | all-to-all | bytes 655360 | tf_op jit(solution)/shard_map/all_to_all | solution.py:436
  51.5 1.0 %unpack.1 = (f32[480,128]{1,0:T(8,128)}, f32[160,128]{1,0:T(8,128)}) custom-call(f32[32,5,4,128]{3,2,1,0:T(4,128)S(1)} %all_to_all.5.recv), custom_call_target="tpu_custom_call" | custom-call | tf_op jit(solution)/shard_map/unpack/pallas_call | solution.py:437
Async XLA Ops:
  0.6 16.7 %copy-start.7 = (f32[1,16,128]{2,1,0:T(8,128)S(1)}, f32[1,16,128]{2,1,0:T(8,128)}, u32[]{:S(2)}) copy-start(f32[1,16,128]{2,1,0:T(8,128)} %param.19) | copy-start | bytes 24580
  0.6 16.7 %copy-start.2 = (f32[1,16,5,128]{3,1,2,0:T(8,128)S(1)}, f32[1,16,5,128]{3,1,2,0:T(8,128)}, u32[]{:S(2)}) copy-start(f32[1,16,5,128]{3,1,2,0:T(8,128)} %param.18) | copy-start | bytes 122884
  0.7 16.7 %copy-start.1 = (f32[1,16,5,128]{3,1,2,0:T(8,128)S(1)}, f32[1,16,5,128]{3,1,2,0:T(8,128)}, u32[]{:S(2)}) copy-start(f32[1,16,5,128]{3,1,2,0:T(8,128)} %param.17) | copy-start | bytes 122884
  0.7 16.7 %copy-start = (f32[1,16,3,5,128]{4,1,3,2,0:T(8,128)S(1)}, f32[1,16,3,5,128]{4,1,3,2,0:T(8,128)}, u32[]{:S(2)}) copy-start(f32[1,16,3,5,128]{4,1,3,2,0:T(8,128)} %param.16) | copy-start | bytes 368644
  0.7 16.7 %copy-start.8 = (f32[1,1024]{1,0:T(1,128)S(1)}, f32[1,1024]{1,0:T(1,128)}, u32[]{:S(2)}) copy-start(f32[1,1024]{1,0:T(1,128)} %param.15) | copy-start | bytes 12292
  0.7 16.7 %copy-start.6 = (f32[1,5,1024]{2,0,1:T(1,128)S(1)}, f32[1,5,1024]{2,0,1:T(1,128)}, u32[]{:S(2)}) copy-start(f32[1,5,1024]{2,0,1:T(1,128)} %param.14) | copy-start | bytes 61444
  0.7 16.7 %copy-start.5 = (f32[1,5,1024]{2,0,1:T(1,128)S(1)}, f32[1,5,1024]{2,0,1:T(1,128)}, u32[]{:S(2)}) copy-start(f32[1,5,1024]{2,0,1:T(1,128)} %param.13) | copy-start | bytes 61444
  0.7 16.7 %copy-start.4 = (f32[1,5,1024]{2,0,1:T(1,128)S(1)}, f32[1,5,1024]{2,0,1:T(1,128)}, u32[]{:S(2)}) copy-start(f32[1,5,1024]{2,0,1:T(1,128)} %param.12) | copy-start | bytes 61444
  0.7 16.7 %copy-start.9 = (s32[1,512,1]{1,2,0:T(1,128)S(1)}, s32[1,512,1]{1,2,0:T(1,128)}, u32[]{:S(2)}) copy-start(s32[1,512,1]{1,2,0:T(1,128)} %param.21) | copy-start | bytes 6148
  3.5 13.9 %collective-permute-start = (f32[472,128]{1,0:T(8,128)}, f32[472,128]{1,0:T(8,128)S(1)}, u32[]{:S(2)}, u32[]{:S(2)}) collective-permute-start(f32[472,128]{1,0:T(8,128)} %get-tuple-element.12), channel_id=1, source_target_pairs={{0,1},{1,2},{2,3},{3,4},{4,5},{5,6},{6,7},{7,8},{8,9},{9,10},{10,1... | collective-permute-start | bytes 725000 | tf_op jit(solution)/shard_map/ppermute | solution.py:37
  6.6 10.7 %collective-permute-start.1 = (f32[376,128]{1,0:T(8,128)}, f32[376,128]{1,0:T(8,128)S(1)}, u32[]{:S(2)}, u32[]{:S(2)}) collective-permute-start(f32[376,128]{1,0:T(8,128)} %get-tuple-element.13), channel_id=1, source_target_pairs={{1,0},{2,1},{3,2},{4,3},{5,4},{6,5},{7,6},{8,7},{9,8},{10,9},{11,1... | collective-permute-start | bytes 577544 | tf_op jit(solution)/shard_map/ppermute | solution.py:37
  13.3 0.8 %copy-start.3 = (f32[5,16,128]{2,1,0:T(8,128)S(1)}, f32[5,16,128]{2,1,0:T(8,128)}, u32[]{:S(2)}) copy-start(f32[5,16,128]{2,1,0:T(8,128)} %get-tuple-element.14.own) | copy-start | bytes 122884
